TPU v7x, 32 devices: a whole 2x2x4 slice. The times are simulated.
32 devices in a mesh: rep: 2 (over x), fsdp: 16 (over z, y, core).
Axes of the slice: x: 2, y: 2, z: 4, core: 2. Of those that a mesh axis runs over, the one named last changes fastest.
Arguments:
- tokens: bfloat16 [256, 128, 768], P(('rep', 'fsdp')), may hold values from -6 to 6
- timesteps: int32 [256], P(('rep', 'fsdp')), may hold values from 0 to 1999
- split_at: int32 [256], P(('rep', 'fsdp')), may hold values from 32 to 96
- sample_weight: float32 [256], P(('rep', 'fsdp')), may hold values from 0.5 to 2
- cotangent: bfloat16 [256, 128, 768], P(('rep', 'fsdp')), may hold values from -6 to 6
- time_w1: bfloat16 [128, 512], P('fsdp'), may hold values from -0.75 to 0.75
- time_w2: bfloat16 [512, 768], P('fsdp'), may hold values from -0.25 to 0.25
- attn_qkv: bfloat16 [768, 2304], P('fsdp'), may hold values from -0.21875 to 0.21875
- attn_out: bfloat16 [768, 768], P('fsdp'), may hold values from -0.875 to 0.875
- ff_in: bfloat16 [768, 3072], P('fsdp'), may hold values from -0.21875 to 0.21875
- ff_out: bfloat16 [3072, 768], P('fsdp'), may hold values from -0.109375 to 0.109375
- biases: bfloat16 [7, 768], P(None, 'fsdp'), may hold values from -3 to 3
- norm_gains: bfloat16 [2, 768], P(None, 'fsdp'), may hold values from 0.5 to 1.5
- ff_bias: bfloat16 [3072], P('fsdp'), may hold values from -3 to 3
- time_bias: bfloat16 [512], P('fsdp'), may hold values from -3 to 3
Outputs:
- output: bfloat16 [256, 128, 768], P(('rep', 'fsdp'))
- grad_tokens: bfloat16 [256, 128, 768], P(('rep', 'fsdp'))
- grad_time_w1: float32 [128, 512], P('fsdp')
- grad_time_w2: float32 [512, 768], P('fsdp')
- grad_attn_qkv: float32 [768, 2304], P('fsdp')
- grad_attn_out: float32 [768, 768], P('fsdp')
- grad_ff_in: float32 [768, 3072], P('fsdp')
- grad_ff_out: float32 [3072, 768], P('fsdp')
- grad_biases: float32 [7, 768], P(None, 'fsdp')
- grad_norm_gains: float32 [2, 768], P(None, 'fsdp')
- grad_ff_bias: float32 [3072], P('fsdp')
- grad_time_bias: float32 [512], P('fsdp')
All inputs are finite; a program needn't handle non-finite values.
Results may differ from a plain program's by a relative error of at most 0.017.
Values may be sent and summed in bfloat16 or wider, within the bound.
No kernel may reach another device: no remote copies, remote signals or barrier semaphores. Data moves between devices by JAX's collectives and lax.ppermute only.
A program may use at most 192 MiB of HBM per device.

v0:
```python
import math

import jax
import jax.numpy as jnp
from jax import lax
from jax.experimental import pallas as pl
from jax.sharding import PartitionSpec as P


HEAD = 64


def precise(left, right):
    return jnp.dot(left, right, precision=lax.Precision.HIGHEST, preferred_element_type=jnp.float32)


def sinusoid(steps_in, width):
    half_width = width // 2
    frequency = jnp.exp(-math.log(10000.0) * jnp.arange(half_width, dtype=jnp.float32) / half_width)
    angles = steps_in.astype(jnp.float32)[:, None] * frequency[None, :]
    return jnp.concatenate([jnp.cos(angles), jnp.sin(angles)], axis=1)


def normalize(values_in, gain_vec, shift_vec):
    center = jnp.mean(values_in, axis=-1, keepdims=True)
    spread = jnp.mean((values_in - center) ** 2, axis=-1, keepdims=True)
    return (values_in - center) * lax.rsqrt(spread + 1e-05) * gain_vec + shift_vec


def contract_rows(left, right):
    return lax.dot_general(
        left, right, (((0,), (0,)), ((), ())), preferred_element_type=jnp.float32
    )


def times_transpose(left, right):
    return lax.dot_general(
        left, right, (((1,), (1,)), ((), ())), preferred_element_type=jnp.float32
    )


def low_dot(left, right, dims):
    return lax.dot_general(left, right, (dims, ((), ())), preferred_element_type=jnp.float32)


def two_heads(block):
    first = lax.broadcasted_iota(jnp.int32, block.shape, 1) < HEAD
    zero = jnp.zeros_like(block)
    return jnp.concatenate([jnp.where(first, block, zero), jnp.where(first, zero, block)], axis=0)


def attend_forward_body(projected_ref, context_ref, attend_ref):
    length, width = context_ref.shape
    pair = 2 * HEAD
    for start in range(0, width, pair):
        queries = projected_ref[:, start : start + pair] * 0.125
        keys = two_heads(projected_ref[:, width + start : width + start + pair])
        values = two_heads(projected_ref[:, 2 * width + start : 2 * width + start + pair])
        scores = low_dot(queries, keys, ((1,), (1,)))
        parts = []
        for half in range(2):
            part = scores[:, half * length : (half + 1) * length]
            part = jnp.exp(part - jnp.max(part, axis=1, keepdims=True))
            parts.append(part * (1.0 / jnp.sum(part, axis=1, keepdims=True)))
        attend = jnp.concatenate(parts, axis=1).astype(jnp.bfloat16)
        context = low_dot(attend, values, ((1,), (0,)))
        context_ref[:, start : start + pair] = context.astype(jnp.bfloat16)
        at = start // HEAD * length
        attend_ref[:, at : at + 2 * length] = attend


def attend_forward(projected, length):
    rows, wide = projected.shape
    width = wide // 3
    kept = width // HEAD * length
    return pl.pallas_call(
        attend_forward_body,
        grid=(rows // length,),
        in_specs=[pl.BlockSpec((length, wide), lambda seq: (seq, 0))],
        out_specs=[
            pl.BlockSpec((length, width), lambda seq: (seq, 0)),
            pl.BlockSpec((length, kept), lambda seq: (seq, 0)),
        ],
        out_shape=[
            jax.ShapeDtypeStruct((rows, width), jnp.bfloat16),
            jax.ShapeDtypeStruct((rows, kept), jnp.bfloat16),
        ],
        name="attend_forward",
    )(projected)


def attend_backward_body(projected_ref, attend_ref, d_context_ref, d_projected_ref, sums_ref):
    length, width = d_context_ref.shape
    pair = 2 * HEAD
    first = lax.broadcasted_iota(jnp.int32, (length, pair), 1) < HEAD
    for start in range(0, width, pair):
        cols = [slice(part * width + start, part * width + start + pair) for part in range(3)]
        queries = projected_ref[:, cols[0]] * 0.125
        keys = two_heads(projected_ref[:, cols[1]] * 0.125)
        values = two_heads(projected_ref[:, cols[2]])
        d_context = d_context_ref[:, start : start + pair]
        at = start // HEAD * length
        attend = attend_ref[:, at : at + 2 * length]
        d_attend = low_dot(d_context, values, ((1,), (1,)))
        raw = []
        for half in range(2):
            place = slice(half * length, (half + 1) * length)
            weights = attend[:, place].astype(jnp.float32)
            slopes = d_attend[:, place]
            total = jnp.sum(weights * slopes, axis=1, keepdims=True)
            raw.append(weights * (slopes - total))
        d_raw = jnp.concatenate(raw, axis=1).astype(jnp.bfloat16)
        d_queries = low_dot(d_raw, keys, ((1,), (0,)))
        both_keys = low_dot(d_raw, queries, ((0,), (0,)))
        both_values = low_dot(attend, d_context, ((0,), (0,)))
        d_keys = jnp.where(first, both_keys[:length], both_keys[length:])
        d_values = jnp.where(first, both_values[:length], both_values[length:])
        d_projected_ref[:, cols[0]] = d_queries.astype(jnp.bfloat16)
        d_projected_ref[:, cols[1]] = d_keys.astype(jnp.bfloat16)
        d_projected_ref[:, cols[2]] = d_values.astype(jnp.bfloat16)
        sums_ref[0, 0:1, start : start + pair] = jnp.sum(d_queries, axis=0, keepdims=True)
        sums_ref[0, 1:2, start : start + pair] = jnp.sum(d_values, axis=0, keepdims=True)


def attend_backward(projected, attend, d_context, length):
    rows, wide = projected.shape
    width = wide // 3
    seqs = rows // length
    return pl.pallas_call(
        attend_backward_body,
        grid=(seqs,),
        in_specs=[
            pl.BlockSpec((length, wide), lambda seq: (seq, 0)),
            pl.BlockSpec((length, attend.shape[1]), lambda seq: (seq, 0)),
            pl.BlockSpec((length, width), lambda seq: (seq, 0)),
        ],
        out_specs=[
            pl.BlockSpec((length, wide), lambda seq: (seq, 0)),
            pl.BlockSpec((1, 2, width), lambda seq: (seq, 0, 0)),
        ],
        out_shape=[
            jax.ShapeDtypeStruct((rows, wide), jnp.bfloat16),
            jax.ShapeDtypeStruct((seqs, 2, width), jnp.float32),
        ],
        name="attend_backward",
    )(projected, attend, d_context)


def swap_bit(count, bit):
    return [(place, place ^ (1 << bit)) for place in range(count)]


def add_up(terms):
    total = terms[0].astype(jnp.float32)
    for term in terms[1:]:
        total = total + term.astype(jnp.float32)
    return total


def reduce_stages(blocks, rep_first):
    count = lax.axis_size("fsdp")
    place = lax.axis_index("fsdp")
    replica = lax.axis_index("rep")
    cross = [(0, 1), (1, 0)]
    half = blocks.shape[-1] // 2
    terms = [blocks]
    left, bit = count, 0
    while left > 1:
        mine = (place >> bit) & 1
        paired = [term.reshape((left // 2, 2) + term.shape[1:]) for term in terms]
        away = [lax.dynamic_index_in_dim(term, 1 - mine, 1, keepdims=False) for term in paired]
        home = [lax.dynamic_index_in_dim(term, mine, 1, keepdims=False) for term in paired]
        sent = add_up(away).astype(jnp.bfloat16)
        terms = home + [lax.ppermute(sent, "fsdp", swap_bit(count, bit))]
        left, bit = left // 2, bit + 1
        if rep_first and bit == 1:
            away = [lax.dynamic_slice_in_dim(term, (1 - replica) * half, half, 2) for term in terms]
            home = [lax.dynamic_slice_in_dim(term, replica * half, half, 2) for term in terms]
            sent = add_up(away).astype(jnp.bfloat16)
            terms = home + [lax.ppermute(sent, "rep", cross)]
    low = add_up(terms)[0].astype(jnp.bfloat16)
    if lax.axis_size("rep") != 2:
        return lax.psum(low, "rep").astype(jnp.float32)
    other = lax.ppermute(low, "rep", cross)
    if not rep_first:
        return low.astype(jnp.float32) + other.astype(jnp.float32)
    pair = [jnp.where(replica == 0, low, other), jnp.where(replica == 0, other, low)]
    return jnp.concatenate(pair, axis=-1).astype(jnp.float32)


def reduce_matrix(grad, rep_first=False):
    count = lax.axis_size("fsdp")
    blocks = grad.astype(jnp.bfloat16).reshape(count, grad.shape[0] // count, grad.shape[1])
    return reduce_stages(blocks, rep_first and lax.axis_size("rep") == 2)


def reduce_small(time_w2_grad, parts):
    count = lax.axis_size("fsdp")
    width = time_w2_grad.shape[1]
    big = time_w2_grad.astype(jnp.bfloat16).reshape(count, -1, width)
    flat = jnp.concatenate([part.astype(jnp.bfloat16) for part in parts], axis=1)
    sizes = [part.shape[1] for part in parts]
    used = sum(sizes)
    rows = -(-used // width)
    flat = jnp.pad(flat, ((0, 0), (0, rows * width - used))).reshape(count, rows, width)
    summed = reduce_stages(jnp.concatenate([big, flat], axis=1), False)
    own_big = summed[: big.shape[1]]
    own_flat = summed[big.shape[1] :].reshape(-1)
    pieces, start = [], 0
    for size in sizes:
        pieces.append(own_flat[start : start + size])
        start += size
    return own_big, pieces


def gather_blocks(shard):
    count = lax.axis_size("fsdp")
    place = lax.axis_index("fsdp")
    held = shard[None]
    for bit in reversed(range(count.bit_length() - 1)):
        other = lax.ppermute(held, "fsdp", swap_bit(count, bit))
        upper = ((place >> bit) & 1) == 1
        pair = [jnp.where(upper, other, held), jnp.where(upper, held, other)]
        held = jnp.stack(pair, axis=1).reshape((2 * held.shape[0],) + held.shape[1:])
    return held


def gather_small(time_w2, parts):
    count = lax.axis_size("fsdp")
    width = time_w2.shape[1]
    flat = jnp.concatenate([part.reshape(-1) for part in parts])
    rows = -(-flat.shape[0] // width)
    flat = jnp.pad(flat, (0, rows * width - flat.shape[0])).reshape(rows, width)
    whole = gather_blocks(jnp.concatenate([time_w2, flat], axis=0))
    full_tw2 = whole[:, : time_w2.shape[0]].reshape(-1, width)
    flat = whole[:, time_w2.shape[0] :].reshape(count, -1)
    pieces, start = [], 0
    for part in parts:
        pieces.append(flat[:, start : start + part.size].reshape((count,) + part.shape))
        start += part.size
    return full_tw2, pieces


def per_device(
    tokens,
    timesteps,
    split_at,
    sample_weight,
    cotangent,
    time_w1,
    time_w2,
    attn_qkv,
    attn_out,
    ff_in,
    ff_out,
    biases,
    norm_gains,
    ff_bias,
    time_bias,
):
    seqs, length, width = tokens.shape
    width_in = attn_qkv.shape[1]
    full_tw2, pieces = gather_small(time_w2, [time_w1, biases, norm_gains, ff_bias, time_bias])
    full_tw1 = pieces[0].reshape(-1, time_w1.shape[1])
    full_bias = pieces[1].swapaxes(0, 1).reshape(biases.shape[0], -1)
    full_gain = pieces[2].swapaxes(0, 1).reshape(norm_gains.shape[0], -1)
    full_ffb = pieces[3].reshape(-1)
    full_tb = pieces[4].reshape(-1)
    full_qkv = gather_blocks(attn_qkv).reshape(-1, width_in)
    full_out = gather_blocks(attn_out).reshape(-1, attn_out.shape[1])
    full_in = gather_blocks(ff_in).reshape(-1, ff_in.shape[1])
    full_down = gather_blocks(ff_out).reshape(-1, ff_out.shape[1])
    bias_rows = full_bias.astype(jnp.float32)
    gain_rows = full_gain.astype(jnp.float32)
    sinus = sinusoid(timesteps, full_tw1.shape[0])
    pre_time = precise(sinus, full_tw1.astype(jnp.float32)) + full_tb.astype(jnp.float32)
    hidden_time, silu_pull = jax.vjp(jax.nn.silu, pre_time)
    temb = precise(hidden_time, full_tw2.astype(jnp.float32)) + bias_rows[0]
    token_rows = (tokens.astype(jnp.float32) + temb[:, None, :]).reshape(seqs * length, width)
    rows_low = token_rows.astype(jnp.bfloat16)
    qkv_bias = jnp.concatenate([bias_rows[1], jnp.zeros((width,), jnp.float32), bias_rows[2]])
    projected = jnp.dot(rows_low, full_qkv, preferred_element_type=jnp.float32) + qkv_bias
    projected = projected.astype(jnp.bfloat16)
    context_low, attend = attend_forward(projected, length)
    resid_attn = (
        token_rows
        + jnp.dot(context_low, full_out, preferred_element_type=jnp.float32)
        + bias_rows[3]
    )
    normed, first_pull = jax.vjp(normalize, resid_attn, gain_rows[0], bias_rows[4])
    normed_low = normed.astype(jnp.bfloat16)
    ff_inner = jnp.dot(normed_low, full_in, preferred_element_type=jnp.float32) + full_ffb.astype(
        jnp.float32
    )
    twice_cdf = 1.0 + lax.erf(ff_inner * math.sqrt(0.5))
    active_low = (0.5 * ff_inner * twice_cdf).astype(jnp.bfloat16)
    density = jnp.exp(-0.5 * ff_inner * ff_inner) * (1.0 / math.sqrt(2.0 * math.pi))
    slope_low = (0.5 * twice_cdf + ff_inner * density).astype(jnp.bfloat16)
    resid_ff = (
        normed + jnp.dot(active_low, full_down, preferred_element_type=jnp.float32) + bias_rows[5]
    )
    output, second_pull = jax.vjp(normalize, resid_ff, gain_rows[1], bias_rows[6])
    positions = lax.iota(jnp.int32, length)
    target_mask = (positions[None, :] >= split_at[:, None]).astype(jnp.float32)
    grad_out = (
        cotangent.astype(jnp.float32) * (sample_weight[:, None] * target_mask)[:, :, None]
    ).reshape(seqs * length, width)
    d_ff, d_gain_two, d_shift_two = second_pull(grad_out)
    d_ffout_bias = jnp.sum(d_ff, axis=0)
    d_ff_low = d_ff.astype(jnp.bfloat16)
    grad_down = contract_rows(active_low, d_ff_low)
    d_active = times_transpose(d_ff_low, full_down)
    d_inner = d_active * slope_low.astype(jnp.float32)
    d_ff_bias = jnp.sum(d_inner, axis=0)
    d_inner_low = d_inner.astype(jnp.bfloat16)
    grad_in = contract_rows(normed_low, d_inner_low)
    d_normed = d_ff + times_transpose(d_inner_low, full_in)
    d_attn, d_gain_one, d_shift_one = first_pull(d_normed)
    d_out_bias = jnp.sum(d_attn, axis=0)
    d_attn_low = d_attn.astype(jnp.bfloat16)
    grad_out_proj = contract_rows(context_low, d_attn_low)
    d_context = times_transpose(d_attn_low, full_out).astype(jnp.bfloat16)
    d_projected_low, bias_sums = attend_backward(projected, attend, d_context, length)
    bias_sums = jnp.sum(bias_sums, axis=0)
    d_query_bias, d_value_bias = bias_sums[0], bias_sums[1]
    grad_qkv = contract_rows(rows_low, d_projected_low)
    d_rows = d_attn + times_transpose(d_projected_low, full_qkv)
    d_rows_seq = d_rows.reshape(seqs, length, width)
    d_temb = jnp.sum(d_rows_seq, axis=1)
    d_temb_bias = jnp.sum(d_temb, axis=0)
    grad_tw2 = precise(hidden_time.T, d_temb)
    d_hidden_time = precise(d_temb, full_tw2.astype(jnp.float32).T)
    (d_pre_time,) = silu_pull(d_hidden_time)
    d_time_bias = jnp.sum(d_pre_time, axis=0)
    grad_tw1 = precise(sinus.T, d_pre_time)
    grad_bias_rows = jnp.stack(
        [
            d_temb_bias,
            d_query_bias,
            d_value_bias,
            d_out_bias,
            d_shift_one,
            d_ffout_bias,
            d_shift_two,
        ]
    )
    grad_gain_rows = jnp.stack([d_gain_one, d_gain_two])
    count = lax.axis_size("fsdp")

    def by_column(rows_in):
        rows_n, cols_n = rows_in.shape
        return rows_in.reshape(rows_n, count, cols_n // count).swapaxes(0, 1).reshape(count, -1)

    share_down = reduce_matrix(grad_down)
    share_in = reduce_matrix(grad_in, rep_first=True)
    share_out = reduce_matrix(grad_out_proj)
    middle = grad_qkv.shape[1] // 2
    share_qkv = jnp.concatenate(
        [reduce_matrix(grad_qkv[:, :middle]), reduce_matrix(grad_qkv[:, middle:], rep_first=True)],
        axis=1,
    )
    share_tw2, pieces = reduce_small(
        grad_tw2,
        [
            grad_tw1.reshape(count, -1),
            by_column(grad_bias_rows),
            by_column(grad_gain_rows),
            d_ff_bias.reshape(count, -1),
            d_time_bias.reshape(count, -1),
        ],
    )
    summed = (
        pieces[0].reshape(time_w1.shape),
        share_tw2,
        share_qkv,
        share_out,
        share_in,
        share_down,
        pieces[1].reshape(biases.shape),
        pieces[2].reshape(norm_gains.shape),
        pieces[3],
        pieces[4],
    )
    output_low = output.reshape(seqs, length, width).astype(jnp.bfloat16)
    grad_tokens = d_rows_seq.astype(jnp.bfloat16)
    return (
        output_low,
        grad_tokens,
        summed[0],
        summed[1],
        summed[2],
        summed[3],
        summed[4],
        summed[5],
        summed[6],
        summed[7],
        summed[8],
        summed[9],
    )


def solution(mesh):
    placed = (
        P(("rep", "fsdp"), None, None),
        P(("rep", "fsdp")),
        P(("rep", "fsdp")),
        P(("rep", "fsdp")),
        P(("rep", "fsdp"), None, None),
        P("fsdp", None),
        P("fsdp", None),
        P("fsdp", None),
        P("fsdp", None),
        P("fsdp", None),
        P("fsdp", None),
        P(None, "fsdp"),
        P(None, "fsdp"),
        P("fsdp"),
        P("fsdp"),
    )
    return jax.shard_map(
        per_device,
        mesh=mesh,
        in_specs=placed,
        out_specs=(
            P(("rep", "fsdp"), None, None),
            P(("rep", "fsdp"), None, None),
            P("fsdp", None),
            P("fsdp", None),
            P("fsdp", None),
            P("fsdp", None),
            P("fsdp", None),
            P("fsdp", None),
            P(None, "fsdp"),
            P(None, "fsdp"),
            P("fsdp"),
            P("fsdp"),
        ),
        check_vma=False,
    )
```

profile of v0, /device:TPU:0, one launch (start us, length us, event | category | flops | bytes accessed | tf_op | source)
XLA Modules:
  0.0 462.8 jit_solution(4603471429127772038)
XLA Ops:
  0.7 4.1 collective-permute-start.16
  9.3 2.8 collective-permute-start
  12.3 2.8 collective-permute-start.12
  16.7 22.5 %collective-permute-done = bf16[1,39,768]{2,1,0:T(8,128)(2,1)S(1)} collective-permute-done((bf16[1,39,768]{2,1,0:T(8,128)(2,1)S(1)}, bf16[1,39,768]{2,1,0:T(8,128)(2,1)S(1)}, u32[]{:S(2)}, u32[]{:S(2)}) %collective-permute-start) | collective-permute-done | bytes 59936 | tf_op jit(solution)/shard_map/ppermute | solution.py:221
  43.1 5.8 %collective-permute-done.1 = bf16[2,39,768]{2,1,0:T(8,128)(2,1)S(1)} collective-permute-done((bf16[2,39,768]{2,1,0:T(8,128)(2,1)S(1)}, bf16[2,39,768]{2,1,0:T(8,128)(2,1)S(1)}, u32[]{:S(2)}, u32[]{:S(2)}) %collective-permute-start.1) | collective-permute-done | bytes 119840 | tf_op jit(solution)/shard_map/ppermute | solution.py:221
  49.0 1.6 collective-permute-start.2
  52.1 1.6 collective-permute-start.10
  56.1 1.8 collective-permute-done.2
  58.2 5.0 %collective-permute-done.10 = bf16[4,48,768]{2,1,0:T(8,128)(2,1)S(1)} collective-permute-done((bf16[4,48,768]{2,1,0:T(8,128)(2,1)S(1)}, bf16[4,48,768]{2,1,0:T(8,128)(2,1)S(1)}, u32[]{:S(2)}, u32[]{:S(2)}) %collective-permute-start.10) | collective-permute-done | bytes 294944 | tf_op jit(solution)/shard_map/ppermute | solution.py:221
  66.8 10.6 %collective-permute-done.17 = bf16[2,192,768]{2,1,0:T(8,128)(2,1)S(1)} collective-permute-done((bf16[2,192,768]{2,1,0:T(8,128)(2,1)S(1)}, bf16[2,192,768]{2,1,0:T(8,128)(2,1)S(1)}, u32[]{:S(2)}, u32[]{:S(2)}) %collective-permute-start.17) | collective-permute-done | bytes 589856 | tf_op jit(solution)/shard_map/ppermute | solution.py:221
  79.1 9.6 %collective-permute-done.13 = bf16[2,48,3072]{2,1,0:T(8,128)(2,1)S(1)} collective-permute-done((bf16[2,48,3072]{2,1,0:T(8,128)(2,1)S(1)}, bf16[2,48,3072]{2,1,0:T(8,128)(2,1)S(1)}, u32[]{:S(2)}, u32[]{:S(2)}) %collective-permute-start.13) | collective-permute-done | bytes 589856 | tf_op jit(solution)/shard_map/ppermute | solution.py:221
  93.3 3.0 fusion.24
  102.5 11.5 %collective-permute-done.18 = bf16[4,192,768]{2,1,0:T(8,128)(2,1)} collective-permute-done((bf16[4,192,768]{2,1,0:T(8,128)(2,1)}, bf16[4,192,768]{2,1,0:T(8,128)(2,1)}, u32[]{:S(2)}, u32[]{:S(2)}) %collective-permute-start.18) | collective-permute-done | bytes 1179680 | tf_op jit(solution)/shard_map/ppermute | solution.py:221
  114.0 1.8 select_bitcast_fusion.7
  117.5 20.6 %collective-permute-done.14 = bf16[4,48,3072]{2,1,0:T(8,128)(2,1)} collective-permute-done((bf16[4,48,3072]{2,1,0:T(8,128)(2,1)}, bf16[4,48,3072]{2,1,0:T(8,128)(2,1)}, u32[]{:S(2)}, u32[]{:S(2)}) %collective-permute-start.14) | collective-permute-done | bytes 1179680 | tf_op jit(solution)/shard_map/ppermute | solution.py:221
  138.2 1.8 select_bitcast_fusion.9
  140.2 1.7 copy.66
  142.8 1.7 copy-done.7
  144.6 5.6 %add_convert_fusion.projected_ref = bf16[1024,2304]{1,0:T(8,128)(2,1)} fusion(bf16[1024,768]{1,0:T(8,128)(2,1)S(1)} %bitcast.477, bf16[768,2304]{1,0:T(8,128)(2,1)S(1)} %bitcast.448, f32[2304]{0:T(1024)S(1)} %pad_maximum_fusion.16), kind=kOutput, calls=%fused_computation.9 | convolution fusion | flops 3628597248 | bytes 9839616 | tf_op jit(solution)/shard_map/dot_general | solution.py:282
  150.2 10.5 %attend_forward.1 = (bf16[1024,768]{1,0:T(8,128)(2,1)}, bf16[1024,1536]{1,0:T(8,128)(2,1)}) custom-call(bf16[1024,2304]{1,0:T(8,128)(2,1)} %add_convert_fusion.projected_ref), custom_call_target="tpu_custom_call" | custom-call | tf_op jit(solution)/shard_map/attend_forward/pallas_call | solution.py:76
  160.6 3.3 fusion.83
  164.4 2.7 select_bitcast_fusion.1
  168.0 2.7 select_bitcast_fusion.3
  171.6 9.7 %multiply_convert_fusion = (bf16[1024,3072]{1,0:T(8,128)(2,1)S(1)}, f32[1024,3072]{1,0:T(8,128)}) fusion(f32[3072]{0:T(1024)S(1)} %reshape.1449, bf16[768,3072]{1,0:T(8,128)(2,1)S(1)} %bitcast.439, f32[1024,768]{1,0:T(8,128)S(1)} %get-tuple-element.108, f32[768]{0:T(1024)S(1)} %add.1063, f32[768]{0:T(1024)S(1)} %mul.234, f32[1024]{0:T(1024)S(1)} %fusion.63, ...), kind=kOutput, calls=%fused_computation.7 | convolution fusion | flops 4854644736 | bytes 26765312 | tf_op jit(solution)/shard_map/dot_general | solution.py:292
  181.3 5.4 %fusion.84 = (f32[1024]{0:T(1024)S(1)}, f32[1024,768]{1,0:T(8,128)S(1)}) fusion(f32[768]{0:T(1024)S(1)} %add.1071, bf16[1024,3072]{1,0:T(8,128)(2,1)S(1)} %get-tuple-element.109, bf16[3072,768]{1,0:T(8,128)(2,1)S(1)} %bitcast.434, f32[768]{0:T(1024)S(1)} %add.1063, f32[768]{0:T(1024)S(1)} %mul.234, f32[1024]{0:T(1024)S(1)} %fusion.63, ...), kind=kOutput, calls=%fused_computation.277 | convolution fusion | flops 4837342208 | bytes 17323008 | tf_op jit(solution)/shard_map/dot_general | solution.py:300
  190.6 3.0 fusion.80
  193.6 7.0 %convolution_convert_fusion = bf16[3072,768]{1,0:T(8,128)(2,1)} fusion(bf16[1024,3072]{1,0:T(8,128)(2,1)S(1)} %get-tuple-element.109, f32[1024,768]{1,0:T(8,128)S(1)} %get-tuple-element.42), kind=kOutput, calls=%fused_computation.12 | convolution fusion | flops 4834983936 | bytes 14155776 | tf_op jit(solution)/shard_map/dot_general | solution.py:31
  200.6 16.5 %fusion.5 = (bf16[3072]{0:T(1024)(128)(2,1)}, bf16[1024,3072]{1,0:T(8,128)(2,1)}, f32[1024,3072]{1,0:T(8,128)}) fusion(f32[1024,3072]{1,0:T(8,128)} %get-tuple-element.110, f32[3072]{0:T(1024)S(1)} %reshape.1449, bf16[3072,768]{1,0:T(8,128)(2,1)S(1)} %bitcast.435, f32[1024,768]{1,0:T(8,128)S(1)} %get-tuple-element.42), kind=kOutput, calls=%fused_computation.10 | convolution fusion | flops 4873516032 | bytes 39340032 | tf_op jit(solution)/shard_map/dot_general | solution.py:37
  217.2 14.2 %convolution_convert_fusion.1 = bf16[768,3072]{1,0:T(8,128)(2,1)} fusion(f32[1024,3072]{1,0:T(8,128)} %get-tuple-element.113, bf16[1024,3072]{1,0:T(8,128)(2,1)} %get-tuple-element.40, f32[1024,768]{1,0:T(8,128)S(1)} %get-tuple-element.108, f32[768]{0:T(1024)S(1)} %add.1063, f32[768]{0:T(1024)S(1)} %mul.234, f32[1024]{0:T(1024)S(1)} %fusion.63, ...), kind=kOutput, calls=%fused_computation.13 | convolution fusion | flops 4847566848 | bytes 26753024 | tf_op jit(solution)/shard_map/dot_general | solution.py:31
  231.3 12.4 %multiply_reduce_fusion = (bf16[768]{0:T(1024)(128)(2,1)S(1)}, f32[1024]{0:T(1024)S(1)}, f32[1024]{0:T(1024)S(1)}, bf16[768]{0:T(1024)(128)(2,1)}, f32[1024,768]{1,0:T(8,128)}) fusion(f32[1024,768]{1,0:T(8,128)S(1)} %get-tuple-element.108, f32[1024]{0:T(1024)S(1)} %fusion.63, f32[1024]{0:T(1024)S(1)} %broadcast_multiply_fusion.1, f32[768]{0:T(1024)S(1)} %mul.234, ...), kind=kOutput, calls=%fused_computation.25 | convolution fusion | flops 4849922048 | bytes 33052672 | tf_op jit(solution)/shard_map/dot_general | solution.py:37
  245.6 1.8 fusion.81
  247.4 2.5 convolution_convert_fusion.4
  249.9 2.6 convolution_convert_fusion.3.d_context_ref
  252.5 18.6 %attend_backward.1 = (bf16[1024,2304]{1,0:T(8,128)(2,1)}, f32[8,2,768]{2,1,0:T(2,128)}) custom-call(bf16[1024,2304]{1,0:T(8,128)(2,1)} %add_convert_fusion.projected_ref, bf16[1024,1536]{1,0:T(8,128)(2,1)} %get-tuple-element.17.attend_ref, bf16[1024,768]{1,0:T(8,128)(2,1)} %convolution_convert_fusion.3.d_context_ref), custom_call_target="tpu_custom_call" | custom-call | tf_op jit(solution)/shard_map/attend_backward/pallas_call | solution.py:129
  271.1 8.3 %bitcast_reduce_fusion = (f32[8,768]{1,0:T(8,128)S(1)}, f32[1024,768]{1,0:T(8,128)S(1)}) fusion(f32[1024,768]{1,0:T(8,128)} %copy-done.9, bf16[1024,2304]{1,0:T(8,128)(2,1)} %get-tuple-element.18, bf16[768,2304]{1,0:T(8,128)(2,1)} %bitcast.449), kind=kOutput, calls=%fused_computation.18 | convolution fusion | flops 3625445376 | bytes 14573568 | tf_op jit(solution)/shard_map/dot_general | solution.py:37
  280.7 2.4 convolution_convert_fusion.5
  283.1 1.8 constant_dynamic-slice_fusion.8
  290.6 4.5 convolution_convert_fusion.2
  298.5 1.6 constant_dynamic-slice_fusion.12
  306.9 1.6 convert_element_type.1064
  310.0 1.7 concatenate.41
  313.3 1.8 concatenate.42
  317.0 2.0 constant_dynamic-slice_fusion.10
  319.9 1.6 collective-permute-start.21
  323.1 5.6 %collective-permute-done.21 = bf16[4,39,768]{2,1,0:T(8,128)(2,1)S(1)} collective-permute-done((bf16[4,39,768]{2,1,0:T(8,128)(2,1)S(1)}, bf16[4,39,768]{2,1,0:T(8,128)(2,1)S(1)}, u32[]{:S(2)}, u32[]{:S(2)}) %collective-permute-start.21) | collective-permute-done | bytes 239648 | tf_op jit(solution)/shard_map/ppermute | solution.py:174
  331.9 1.8 collective-permute-done.22
  334.1 2.1 collective-permute-start.23
  336.3 2.1 collective-permute-start.38
  338.4 1.9 fusion.28
  340.3 1.8 constant_dynamic-slice_fusion.11
  345.6 2.4 fusion.13
  349.7 5.4 %collective-permute-done.39 = bf16[1,48,768]{2,1,0:T(8,128)(2,1)S(1)} collective-permute-done((bf16[1,48,768]{2,1,0:T(8,128)(2,1)S(1)}, bf16[1,48,768]{2,1,0:T(8,128)(2,1)S(1)}, u32[]{:S(2)}, u32[]{:S(2)}) %collective-permute-start.39) | collective-permute-done | bytes 73760 | tf_op jit(solution)/shard_map/ppermute | solution.py:174
  355.7 6.3 %collective-permute-done.24 = bf16[39,768]{1,0:T(8,128)(2,1)S(1)} collective-permute-done((bf16[39,768]{1,0:T(8,128)(2,1)S(1)}, bf16[39,768]{1,0:T(8,128)(2,1)S(1)}, u32[]{:S(2)}, u32[]{:S(2)}) %collective-permute-start.24) | collective-permute-done | bytes 59936 | tf_op jit(solution)/shard_map/ppermute | solution.py:184
  372.3 3.0 collective-permute-done.27
  377.2 1.8 collective-permute-start.33
  378.9 4.3 collective-permute-done.28
  385.0 2.0 fusion.10
  394.0 19.5 %collective-permute-done.35 = bf16[48,576]{1,0:T(8,128)(2,1)S(1)} collective-permute-done((bf16[48,576]{1,0:T(8,128)(2,1)S(1)}, bf16[48,576]{1,0:T(8,128)(2,1)S(1)}, u32[]{:S(2)}, u32[]{:S(2)}) %collective-permute-start.35) | collective-permute-done | bytes 55328 | tf_op jit(solution)/shard_map/ppermute | solution.py:184
  418.4 10.2 %collective-permute-done.43 = bf16[4,48,1536]{2,1,0:T(8,128)(2,1)S(1)} collective-permute-done((bf16[4,48,1536]{2,1,0:T(8,128)(2,1)S(1)}, bf16[4,48,1536]{2,1,0:T(8,128)(2,1)S(1)}, u32[]{:S(2)}, u32[]{:S(2)}) %collective-permute-start.43) | collective-permute-done | bytes 589856 | tf_op jit(solution)/shard_map/ppermute | solution.py:174
  428.8 7.1 %collective-permute-done.44 = bf16[2,48,1536]{2,1,0:T(8,128)(2,1)S(1)} collective-permute-done((bf16[2,48,1536]{2,1,0:T(8,128)(2,1)S(1)}, bf16[2,48,1536]{2,1,0:T(8,128)(2,1)S(1)}, u32[]{:S(2)}, u32[]{:S(2)}) %collective-permute-start.44) | collective-permute-done | bytes 294944 | tf_op jit(solution)/shard_map/ppermute | solution.py:174
  436.0 1.8 collective-permute-start.45
  440.0 9.1 %collective-permute-done.45 = bf16[1,48,1536]{2,1,0:T(8,128)(2,1)S(1)} collective-permute-done((bf16[1,48,1536]{2,1,0:T(8,128)(2,1)S(1)}, bf16[1,48,1536]{2,1,0:T(8,128)(2,1)S(1)}, u32[]{:S(2)}, u32[]{:S(2)}) %collective-permute-start.45) | collective-permute-done | bytes 147488 | tf_op jit(solution)/shard_map/ppermute | solution.py:174
  450.7 3.2 collective-permute-done.50
  456.4 5.1 %collective-permute-done.51 = bf16[192,768]{1,0:T(8,128)(2,1)S(1)} collective-permute-done((bf16[192,768]{1,0:T(8,128)(2,1)S(1)}, bf16[192,768]{1,0:T(8,128)(2,1)S(1)}, u32[]{:S(2)}, u32[]{:S(2)}) %collective-permute-start.51) | collective-permute-done | bytes 294944 | tf_op jit(solution)/shard_map/ppermute | solution.py:184
  (348 shorter events, 108.1 us)
Async XLA Ops:
  0.6 53.1 %copy-start.26 = (bf16[192,768]{1,0:T(8,128)(2,1)S(1)}, bf16[192,768]{1,0:T(8,128)(2,1)}, u32[]{:S(2)}) copy-start(bf16[192,768]{1,0:T(8,128)(2,1)} %param.25) | copy-start | bytes 884740
  0.7 53.1 %collective-permute-start.16 = (bf16[1,192,768]{2,1,0:T(8,128)(2,1)}, bf16[1,192,768]{2,1,0:T(8,128)(2,1)S(1)}, u32[]{:S(2)}, u32[]{:S(2)}) collective-permute-start(bf16[1,192,768]{2,1,0:T(8,128)(2,1)} %bitcast.521), channel_id=1, source_target_pairs={{0,8},{1,9},{2,10},{3,11},{4,12},{5,13},{6,14},{7,15},{8,0},{9,1},... | collective-permute-start | bytes 884744 | tf_op jit(solution)/shard_map/ppermute | solution.py:221
  4.8 45.9 %collective-permute-start.4 = (bf16[1,48,2304]{2,1,0:T(8,128)(2,1)}, bf16[1,48,2304]{2,1,0:T(8,128)(2,1)S(1)}, u32[]{:S(2)}, u32[]{:S(2)}) collective-permute-start(bf16[1,48,2304]{2,1,0:T(8,128)(2,1)} %bitcast.533), channel_id=1, source_target_pairs={{0,8},{1,9},{2,10},{3,11},{4,12},{5,13},{6,14},{7,15},{8,0},{9,1},... | collective-permute-start | bytes 663560 | tf_op jit(solution)/shard_map/ppermute | solution.py:221
  9.3 29.8 %collective-permute-start = (bf16[1,39,768]{2,1,0:T(8,128)(2,1)S(1)}, bf16[1,39,768]{2,1,0:T(8,128)(2,1)S(1)}, u32[]{:S(2)}, u32[]{:S(2)}) collective-permute-start(bf16[1,39,768]{2,1,0:T(8,128)(2,1)S(1)} %maximum_bitcast_fusion.5), channel_id=1, source_target_pairs={{0,8},{1,9},{2,10},{3,11},{4,12},{5,13},{6,14},{7,15},{8,0},{9,1},... | collective-permute-start | bytes 179720 | tf_op jit(solution)/shard_map/ppermute | solution.py:221
  12.2 28.6 %collective-permute-start.8 = (bf16[1,48,768]{2,1,0:T(8,128)(2,1)}, bf16[1,48,768]{2,1,0:T(8,128)(2,1)S(1)}, u32[]{:S(2)}, u32[]{:S(2)}) collective-permute-start(bf16[1,48,768]{2,1,0:T(8,128)(2,1)} %bitcast.534), channel_id=1, source_target_pairs={{0,8},{1,9},{2,10},{3,11},{4,12},{5,13},{6,14},{7,15},{8,0},{9,1},... | collective-permute-start | bytes 221192 | tf_op jit(solution)/shard_map/ppermute | solution.py:221
  12.3 42.3 %collective-permute-start.12 = (bf16[1,48,3072]{2,1,0:T(8,128)(2,1)}, bf16[1,48,3072]{2,1,0:T(8,128)(2,1)S(1)}, u32[]{:S(2)}, u32[]{:S(2)}) collective-permute-start(bf16[1,48,3072]{2,1,0:T(8,128)(2,1)} %bitcast.522), channel_id=1, source_target_pairs={{0,8},{1,9},{2,10},{3,11},{4,12},{5,13},{6,14},{7,15},{8,0},{9,1},... | collective-permute-start | bytes 884744 | tf_op jit(solution)/shard_map/ppermute | solution.py:221
  15.9 76.1 %copy-start.32 = (f32[8,64]{1,0:T(8,128)}, f32[8,64]{1,0:T(8,128)S(1)}, u32[]{:S(2)}) copy-start(f32[8,64]{1,0:T(8,128)S(1)} %get-tuple-element.105) | copy-start | bytes 6148
  15.9 76.1 %copy-start.34 = (f32[8,64]{1,0:T(8,128)}, f32[8,64]{1,0:T(8,128)S(1)}, u32[]{:S(2)}) copy-start(f32[8,64]{1,0:T(8,128)S(1)} %get-tuple-element.106) | copy-start | bytes 6148
  40.0 8.9 %collective-permute-start.1 = (bf16[2,39,768]{2,1,0:T(8,128)(2,1)S(1)}, bf16[2,39,768]{2,1,0:T(8,128)(2,1)S(1)}, u32[]{:S(2)}, u32[]{:S(2)}) collective-permute-start(bf16[2,39,768]{2,1,0:T(8,128)(2,1)S(1)} %maximum_bitcast_fusion.4), channel_id=1, source_target_pairs={{0,4},{1,5},{2,6},{3,7},{4,0},{5,1},{6,2},{7,3},{8,12},{9,13},{10,... | collective-permute-start | bytes 359432 | tf_op jit(solution)/shard_map/ppermute | solution.py:221
  41.7 12.9 %copy-start.27 = (bf16[48,3072]{1,0:T(8,128)(2,1)S(1)}, bf16[48,3072]{1,0:T(8,128)(2,1)}, u32[]{:S(2)}) copy-start(bf16[48,3072]{1,0:T(8,128)(2,1)} %param.24) | copy-start | bytes 884740
  41.7 10.3 %collective-permute-start.9 = (bf16[2,48,768]{2,1,0:T(8,128)(2,1)S(1)}, bf16[2,48,768]{2,1,0:T(8,128)(2,1)S(1)}, u32[]{:S(2)}, u32[]{:S(2)}) collective-permute-start(bf16[2,48,768]{2,1,0:T(8,128)(2,1)S(1)} %maximum_bitcast_fusion.3), channel_id=1, source_target_pairs={{0,4},{1,5},{2,6},{3,7},{4,0},{5,1},{6,2},{7,3},{8,12},{9,13},{10,... | collective-permute-start | bytes 442376 | tf_op jit(solution)/shard_map/ppermute | solution.py:221
  49.0 8.9 %collective-permute-start.2 = (bf16[4,39,768]{2,1,0:T(8,128)(2,1)S(1)}, bf16[4,39,768]{2,1,0:T(8,128)(2,1)S(1)}, u32[]{:S(2)}, u32[]{:S(2)}) collective-permute-start(bf16[4,39,768]{2,1,0:T(8,128)(2,1)S(1)} %bitcast.509), channel_id=1, source_target_pairs={{0,2},{1,3},{2,0},{3,1},{4,6},{5,7},{6,4},{7,5},{8,10},{9,11},{10,... | collective-permute-start | bytes 718856 | tf_op jit(solution)/shard_map/ppermute | solution.py:221
  51.7 13.1 %collective-permute-start.5 = (bf16[2,48,2304]{2,1,0:T(8,128)(2,1)S(1)}, bf16[2,48,2304]{2,1,0:T(8,128)(2,1)S(1)}, u32[]{:S(2)}, u32[]{:S(2)}) collective-permute-start(bf16[2,48,2304]{2,1,0:T(8,128)(2,1)S(1)} %maximum_bitcast_fusion.2), channel_id=1, source_target_pairs={{0,4},{1,5},{2,6},{3,7},{4,0},{5,1},{6,2},{7,3},{8,12},{9,13},{10,... | collective-permute-start | bytes 1327112 | tf_op jit(solution)/shard_map/ppermute | solution.py:221
  52.1 11.1 %collective-permute-start.10 = (bf16[4,48,768]{2,1,0:T(8,128)(2,1)S(1)}, bf16[4,48,768]{2,1,0:T(8,128)(2,1)S(1)}, u32[]{:S(2)}, u32[]{:S(2)}) collective-permute-start(bf16[4,48,768]{2,1,0:T(8,128)(2,1)S(1)} %bitcast.487), channel_id=1, source_target_pairs={{0,2},{1,3},{2,0},{3,1},{4,6},{5,7},{6,4},{7,5},{8,10},{9,11},{10,... | collective-permute-start | bytes 884744 | tf_op jit(solution)/shard_map/ppermute | solution.py:221
  53.9 23.6 %collective-permute-start.17 = (bf16[2,192,768]{2,1,0:T(8,128)(2,1)S(1)}, bf16[2,192,768]{2,1,0:T(8,128)(2,1)S(1)}, u32[]{:S(2)}, u32[]{:S(2)}) collective-permute-start(bf16[2,192,768]{2,1,0:T(8,128)(2,1)S(1)} %maximum_bitcast_fusion.1), channel_id=1, source_target_pairs={{0,4},{1,5},{2,6},{3,7},{4,0},{5,1},{6,2},{7,3},{8,12},{9,13},{10,... | collective-permute-start | bytes 1769480 | tf_op jit(solution)/shard_map/ppermute | solution.py:221
  54.7 34.1 %collective-permute-start.13 = (bf16[2,48,3072]{2,1,0:T(8,128)(2,1)S(1)}, bf16[2,48,3072]{2,1,0:T(8,128)(2,1)S(1)}, u32[]{:S(2)}, u32[]{:S(2)}) collective-permute-start(bf16[2,48,3072]{2,1,0:T(8,128)(2,1)S(1)} %maximum_bitcast_fusion), channel_id=1, source_target_pairs={{0,4},{1,5},{2,6},{3,7},{4,0},{5,1},{6,2},{7,3},{8,12},{9,13},{10,... | collective-permute-start | bytes 1769480 | tf_op jit(solution)/shard_map/ppermute | solution.py:221
  58.1 32.3 %collective-permute-start.3 = (bf16[8,39,768]{2,1,0:T(8,128)(2,1)S(1)}, bf16[8,39,768]{2,1,0:T(8,128)(2,1)S(1)}, u32[]{:S(2)}, u32[]{:S(2)}) collective-permute-start(bf16[8,39,768]{2,1,0:T(8,128)(2,1)S(1)} %bitcast.468), channel_id=1, source_target_pairs={{0,1},{1,0},{2,3},{3,2},{4,5},{5,4},{6,7},{7,6},{8,9},{9,8},{10,11... | collective-permute-start | bytes 1437704 | tf_op jit(solution)/shard_map/ppermute | solution.py:221
  64.2 33.8 %collective-permute-start.11 = (bf16[8,48,768]{2,1,0:T(8,128)(2,1)}, bf16[8,48,768]{2,1,0:T(8,128)(2,1)}, u32[]{:S(2)}, u32[]{:S(2)}) collective-permute-start(bf16[8,48,768]{2,1,0:T(8,128)(2,1)} %bitcast.42), channel_id=1, source_target_pairs={{0,1},{1,0},{2,3},{3,2},{4,5},{5,4},{6,7},{7,6},{8,9},{9,8},{10,11... | collective-permute-start | bytes 1769480 | tf_op jit(solution)/shard_map/ppermute | solution.py:221
  65.8 33.5 %collective-permute-start.6 = (bf16[4,48,2304]{2,1,0:T(8,128)(2,1)}, bf16[4,48,2304]{2,1,0:T(8,128)(2,1)}, u32[]{:S(2)}, u32[]{:S(2)}) collective-permute-start(bf16[4,48,2304]{2,1,0:T(8,128)(2,1)} %bitcast.25), channel_id=1, source_target_pairs={{0,2},{1,3},{2,0},{3,1},{4,6},{5,7},{6,4},{7,5},{8,10},{9,11},{10,... | collective-permute-start | bytes 2654216 | tf_op jit(solution)/shard_map/ppermute | solution.py:221
  78.7 35.3 %collective-permute-start.18 = (bf16[4,192,768]{2,1,0:T(8,128)(2,1)}, bf16[4,192,768]{2,1,0:T(8,128)(2,1)}, u32[]{:S(2)}, u32[]{:S(2)}) collective-permute-start(bf16[4,192,768]{2,1,0:T(8,128)(2,1)} %bitcast.68), channel_id=1, source_target_pairs={{0,2},{1,3},{2,0},{3,1},{4,6},{5,7},{6,4},{7,5},{8,10},{9,11},{10,... | collective-permute-start | bytes 3538952 | tf_op jit(solution)/shard_map/ppermute | solution.py:221
  90.0 48.2 %collective-permute-start.14 = (bf16[4,48,3072]{2,1,0:T(8,128)(2,1)}, bf16[4,48,3072]{2,1,0:T(8,128)(2,1)}, u32[]{:S(2)}, u32[]{:S(2)}) collective-permute-start(bf16[4,48,3072]{2,1,0:T(8,128)(2,1)} %bitcast.54), channel_id=1, source_target_pairs={{0,2},{1,3},{2,0},{3,1},{4,6},{5,7},{6,4},{7,5},{8,10},{9,11},{10,... | collective-permute-start | bytes 3538952 | tf_op jit(solution)/shard_map/ppermute | solution.py:221
  101.2 40.7 %collective-permute-start.7 = (bf16[8,48,2304]{2,1,0:T(8,128)(2,1)S(1)}, bf16[8,48,2304]{2,1,0:T(8,128)(2,1)S(1)}, u32[]{:S(2)}, u32[]{:S(2)}) collective-permute-start(bf16[8,48,2304]{2,1,0:T(8,128)(2,1)S(1)} %bitcast.420), channel_id=1, source_target_pairs={{0,1},{1,0},{2,3},{3,2},{4,5},{5,4},{6,7},{7,6},{8,9},{9,8},{10,11... | collective-permute-start | bytes 5308424 | tf_op jit(solution)/shard_map/ppermute | solution.py:221
  117.5 46.9 %collective-permute-start.19 = (bf16[8,192,768]{2,1,0:T(8,128)(2,1)}, bf16[8,192,768]{2,1,0:T(8,128)(2,1)}, u32[]{:S(2)}, u32[]{:S(2)}) collective-permute-start(bf16[8,192,768]{2,1,0:T(8,128)(2,1)} %bitcast.71), channel_id=1, source_target_pairs={{0,1},{1,0},{2,3},{3,2},{4,5},{5,4},{6,7},{7,6},{8,9},{9,8},{10,11... | collective-permute-start | bytes 7077896 | tf_op jit(solution)/shard_map/ppermute | solution.py:221
  141.8 26.2 %collective-permute-start.15 = (bf16[8,48,3072]{2,1,0:T(8,128)(2,1)}, bf16[8,48,3072]{2,1,0:T(8,128)(2,1)}, u32[]{:S(2)}, u32[]{:S(2)}) collective-permute-start(bf16[8,48,3072]{2,1,0:T(8,128)(2,1)} %bitcast.57), channel_id=1, source_target_pairs={{0,1},{1,0},{2,3},{3,2},{4,5},{5,4},{6,7},{7,6},{8,9},{9,8},{10,11... | collective-permute-start | bytes 7077896 | tf_op jit(solution)/shard_map/ppermute | solution.py:221
  271.1 12.1 %slice-start = ((s8[4718592]{0:T(1024)(128)(4,1)}), s8[4194304]{0:T(1024)(128)(4,1)S(1)}, s32[]{:S(2)}) async-start(s8[4718592]{0:T(1024)(128)(4,1)} %bitcast.436), calls=%async_computation | async-start | bytes 8388608
  284.9 106.9 %collective-permute-start.47 = (bf16[8,192,768]{2,1,0:T(8,128)(2,1)}, bf16[8,192,768]{2,1,0:T(8,128)(2,1)}, u32[]{:S(2)}, u32[]{:S(2)}) collective-permute-start(bf16[8,192,768]{2,1,0:T(8,128)(2,1)} %get-tuple-element.46), channel_id=1, source_target_pairs={{0,1},{1,0},{2,3},{3,2},{4,5},{5,4},{6,7},{7,6},{8,9},{9,8},{10,11... | collective-permute-start | bytes 7077896 | tf_op jit(solution)/shard_map/ppermute | solution.py:174
  287.9 33.7 %collective-permute-start.36 = (bf16[8,48,768]{2,1,0:T(8,128)(2,1)}, bf16[8,48,768]{2,1,0:T(8,128)(2,1)}, u32[]{:S(2)}, u32[]{:S(2)}) collective-permute-start(bf16[8,48,768]{2,1,0:T(8,128)(2,1)} %get-tuple-element.68), channel_id=1, source_target_pairs={{0,1},{1,0},{2,3},{3,2},{4,5},{5,4},{6,7},{7,6},{8,9},{9,8},{10,11... | collective-permute-start | bytes 1769480 | tf_op jit(solution)/shard_map/ppermute | solution.py:174
  290.6 45.6 %copy-start.22 = (bf16[4,1,48,768]{3,2,1,0:T(8,128)(2,1)}, bf16[4,1,48,768]{3,2,1,0:T(8,128)(2,1)S(1)}, u32[]{:S(2)}) copy-start(bf16[4,1,48,768]{3,2,1,0:T(8,128)(2,1)S(1)} %constant_dynamic-slice_fusion.16) | copy-start | bytes 884740
  296.9 39.4 %collective-permute-start.25 = (bf16[8,48,1152]{2,1,0:T(8,128)(2,1)}, bf16[8,48,1152]{2,1,0:T(8,128)(2,1)}, u32[]{:S(2)}, u32[]{:S(2)}) collective-permute-start(bf16[8,48,1152]{2,1,0:T(8,128)(2,1)} %get-tuple-element.61), channel_id=1, source_target_pairs={{0,1},{1,0},{2,3},{3,2},{4,5},{5,4},{6,7},{7,6},{8,9},{9,8},{10,11... | collective-permute-start | bytes 2654216 | tf_op jit(solution)/shard_map/ppermute | solution.py:174
  298.5 43.6 %collective-permute-start.30 = (bf16[8,48,1152]{2,1,0:T(8,128)(2,1)}, bf16[8,48,1152]{2,1,0:T(8,128)(2,1)}, u32[]{:S(2)}, u32[]{:S(2)}) collective-permute-start(bf16[8,48,1152]{2,1,0:T(8,128)(2,1)} %dynamic-slice_bitcast_fusion.2), channel_id=1, source_target_pairs={{0,1},{1,0},{2,3},{3,2},{4,5},{5,4},{6,7},{7,6},{8,9},{9,8},{10,11... | collective-permute-start | bytes 2654216 | tf_op jit(solution)/shard_map/ppermute | solution.py:174
  315.1 13.8 %copy-start.15 = (bf16[8,1,48,576]{3,2,1,0:T(8,128)(2,1)S(1)}, bf16[8,1,48,576]{3,2,1,0:T(8,128)(2,1)}, u32[]{:S(2)}) copy-start(bf16[8,1,48,576]{3,2,1,0:T(8,128)(2,1)} %constant_dynamic-slice_fusion.5) | copy-start | bytes 1327108
  316.5 3.3 collective-permute-start.20
  319.9 8.9 %collective-permute-start.21 = (bf16[4,39,768]{2,1,0:T(8,128)(2,1)S(1)}, bf16[4,39,768]{2,1,0:T(8,128)(2,1)S(1)}, u32[]{:S(2)}, u32[]{:S(2)}) collective-permute-start(bf16[4,39,768]{2,1,0:T(8,128)(2,1)S(1)} %fusion.35), channel_id=1, source_target_pairs={{0,2},{1,3},{2,0},{3,1},{4,6},{5,7},{6,4},{7,5},{8,10},{9,11},{10,... | collective-permute-start | bytes 718856 | tf_op jit(solution)/shard_map/ppermute | solution.py:174
  322.6 11.5 %collective-permute-start.37 = (bf16[4,48,768]{2,1,0:T(8,128)(2,1)S(1)}, bf16[4,48,768]{2,1,0:T(8,128)(2,1)S(1)}, u32[]{:S(2)}, u32[]{:S(2)}) collective-permute-start(bf16[4,48,768]{2,1,0:T(8,128)(2,1)S(1)} %fusion.29), channel_id=1, source_target_pairs={{0,2},{1,3},{2,0},{3,1},{4,6},{5,7},{6,4},{7,5},{8,10},{9,11},{10,... | collective-permute-start | bytes 884744 | tf_op jit(solution)/shard_map/ppermute | solution.py:174
  328.8 4.9 %collective-permute-start.22 = (bf16[2,39,768]{2,1,0:T(8,128)(2,1)S(1)}, bf16[2,39,768]{2,1,0:T(8,128)(2,1)S(1)}, u32[]{:S(2)}, u32[]{:S(2)}) collective-permute-start(bf16[2,39,768]{2,1,0:T(8,128)(2,1)S(1)} %fusion.46), channel_id=1, source_target_pairs={{0,4},{1,5},{2,6},{3,7},{4,0},{5,1},{6,2},{7,3},{8,12},{9,13},{10,... | collective-permute-start | bytes 359432 | tf_op jit(solution)/shard_map/ppermute | solution.py:174
  333.8 51.3 %collective-permute-start.41 = (bf16[8,48,3072]{2,1,0:T(8,128)(2,1)}, bf16[8,48,3072]{2,1,0:T(8,128)(2,1)S(1)}, u32[]{:S(2)}, u32[]{:S(2)}) collective-permute-start(bf16[8,48,3072]{2,1,0:T(8,128)(2,1)} %dynamic-slice_bitcast_fusion.1), channel_id=1, source_target_pairs={{0,1},{1,0},{2,3},{3,2},{4,5},{5,4},{6,7},{7,6},{8,9},{9,8},{10,11... | collective-permute-start | bytes 7077896 | tf_op jit(solution)/shard_map/ppermute | solution.py:174
  334.1 15.4 %collective-permute-start.23 = (bf16[1,39,768]{2,1,0:T(8,128)(2,1)S(1)}, bf16[1,39,768]{2,1,0:T(8,128)(2,1)S(1)}, u32[]{:S(2)}, u32[]{:S(2)}) collective-permute-start(bf16[1,39,768]{2,1,0:T(8,128)(2,1)S(1)} %fusion.51), channel_id=1, source_target_pairs={{0,8},{1,9},{2,10},{3,11},{4,12},{5,13},{6,14},{7,15},{8,0},{9,1},... | collective-permute-start | bytes 179720 | tf_op jit(solution)/shard_map/ppermute | solution.py:174
  336.3 13.2 %copy-start.23 = (bf16[4,1,48,768]{3,2,1,0:T(8,128)(2,1)S(1)}, bf16[4,1,48,768]{3,2,1,0:T(8,128)(2,1)}, u32[]{:S(2)}) copy-start(bf16[4,1,48,768]{3,2,1,0:T(8,128)(2,1)} %copy-done.22) | copy-start | bytes 884740
  336.3 11.7 %collective-permute-start.38 = (bf16[2,48,768]{2,1,0:T(8,128)(2,1)S(1)}, bf16[2,48,768]{2,1,0:T(8,128)(2,1)S(1)}, u32[]{:S(2)}, u32[]{:S(2)}) collective-permute-start(bf16[2,48,768]{2,1,0:T(8,128)(2,1)S(1)} %fusion.41), channel_id=1, source_target_pairs={{0,4},{1,5},{2,6},{3,7},{4,0},{5,1},{6,2},{7,3},{8,12},{9,13},{10,... | collective-permute-start | bytes 442376 | tf_op jit(solution)/shard_map/ppermute | solution.py:174
  342.1 27.7 %copy-start.16 = (bf16[8,1,48,576]{3,2,1,0:T(8,128)(2,1)S(1)}, bf16[8,1,48,576]{3,2,1,0:T(8,128)(2,1)}, u32[]{:S(2)}) copy-start(bf16[8,1,48,576]{3,2,1,0:T(8,128)(2,1)} %constant_dynamic-slice_fusion.5) | copy-start | bytes 1327108
  342.1 26.0 %collective-permute-start.26 = (bf16[4,48,1152]{2,1,0:T(8,128)(2,1)}, bf16[4,48,1152]{2,1,0:T(8,128)(2,1)}, u32[]{:S(2)}, u32[]{:S(2)}) collective-permute-start(bf16[4,48,1152]{2,1,0:T(8,128)(2,1)} %fusion.28), channel_id=1, source_target_pairs={{0,2},{1,3},{2,0},{3,1},{4,6},{5,7},{6,4},{7,5},{8,10},{9,11},{10,... | collective-permute-start | bytes 1327112 | tf_op jit(solution)/shard_map/ppermute | solution.py:174
  348.0 21.8 %collective-permute-start.31 = (bf16[8,48,576]{2,1,0:T(8,128)(2,1)}, bf16[8,48,576]{2,1,0:T(8,128)(2,1)}, u32[]{:S(2)}, u32[]{:S(2)}) collective-permute-start(bf16[8,48,576]{2,1,0:T(8,128)(2,1)} %fusion.13), channel_id=1, source_target_pairs={{0,16},{16,0},{1,17},{17,1},{2,18},{18,2},{3,19},{19,3},{4,20},{20... | collective-permute-start | bytes 1327112 | tf_op jit(solution)/shard_map/ppermute | solution.py:180
  349.5 5.6 %collective-permute-start.39 = (bf16[1,48,768]{2,1,0:T(8,128)(2,1)S(1)}, bf16[1,48,768]{2,1,0:T(8,128)(2,1)S(1)}, u32[]{:S(2)}, u32[]{:S(2)}) collective-permute-start(bf16[1,48,768]{2,1,0:T(8,128)(2,1)S(1)} %fusion.43), channel_id=1, source_target_pairs={{0,8},{1,9},{2,10},{3,11},{4,12},{5,13},{6,14},{7,15},{8,0},{9,1},... | collective-permute-start | bytes 221192 | tf_op jit(solution)/shard_map/ppermute | solution.py:174
  355.1 6.9 %collective-permute-start.24 = (bf16[39,768]{1,0:T(8,128)(2,1)S(1)}, bf16[39,768]{1,0:T(8,128)(2,1)S(1)}, u32[]{:S(2)}, u32[]{:S(2)}) collective-permute-start(bf16[39,768]{1,0:T(8,128)(2,1)S(1)} %fusion.56), channel_id=1, source_target_pairs={{0,16},{16,0},{1,17},{17,1},{2,18},{18,2},{3,19},{19,3},{4,20},{20... | collective-permute-start | bytes 179720 | tf_op jit(solution)/shard_map/ppermute | solution.py:184
  362.0 5.4 %collective-permute-start.40 = (bf16[48,768]{1,0:T(8,128)(2,1)S(1)}, bf16[48,768]{1,0:T(8,128)(2,1)S(1)}, u32[]{:S(2)}, u32[]{:S(2)}) collective-permute-start(bf16[48,768]{1,0:T(8,128)(2,1)S(1)} %fusion.55), channel_id=1, source_target_pairs={{0,16},{16,0},{1,17},{17,1},{2,18},{18,2},{3,19},{19,3},{4,20},{20... | collective-permute-start | bytes 221192 | tf_op jit(solution)/shard_map/ppermute | solution.py:184
  369.4 6.0 %collective-permute-start.27 = (bf16[2,48,1152]{2,1,0:T(8,128)(2,1)S(1)}, bf16[2,48,1152]{2,1,0:T(8,128)(2,1)S(1)}, u32[]{:S(2)}, u32[]{:S(2)}) collective-permute-start(bf16[2,48,1152]{2,1,0:T(8,128)(2,1)S(1)} %fusion.37), channel_id=1, source_target_pairs={{0,4},{1,5},{2,6},{3,7},{4,0},{5,1},{6,2},{7,3},{8,12},{9,13},{10,... | collective-permute-start | bytes 663560 | tf_op jit(solution)/shard_map/ppermute | solution.py:174
  370.8 6.3 %collective-permute-start.32 = (bf16[4,48,576]{2,1,0:T(8,128)(2,1)S(1)}, bf16[4,48,576]{2,1,0:T(8,128)(2,1)S(1)}, u32[]{:S(2)}, u32[]{:S(2)}) collective-permute-start(bf16[4,48,576]{2,1,0:T(8,128)(2,1)S(1)} %fusion.36), channel_id=1, source_target_pairs={{0,2},{1,3},{2,0},{3,1},{4,6},{5,7},{6,4},{7,5},{8,10},{9,11},{10,... | collective-permute-start | bytes 663560 | tf_op jit(solution)/shard_map/ppermute | solution.py:174
  372.3 19.4 %copy-start.1 = (bf16[8,1,192,768]{3,2,1,0:T(8,128)(2,1)S(1)}, bf16[8,1,192,768]{3,2,1,0:T(8,128)(2,1)}, u32[]{:S(2)}) copy-start(bf16[8,1,192,768]{3,2,1,0:T(8,128)(2,1)} %copy-done) | copy-start | bytes 7077892
  376.4 6.8 %collective-permute-start.28 = (bf16[1,48,1152]{2,1,0:T(8,128)(2,1)S(1)}, bf16[1,48,1152]{2,1,0:T(8,128)(2,1)S(1)}, u32[]{:S(2)}, u32[]{:S(2)}) collective-permute-start(bf16[1,48,1152]{2,1,0:T(8,128)(2,1)S(1)} %fusion.38), channel_id=1, source_target_pairs={{0,8},{1,9},{2,10},{3,11},{4,12},{5,13},{6,14},{7,15},{8,0},{9,1},... | collective-permute-start | bytes 331784 | tf_op jit(solution)/shard_map/ppermute | solution.py:174
  377.2 7.7 %collective-permute-start.33 = (bf16[2,48,576]{2,1,0:T(8,128)(2,1)S(1)}, bf16[2,48,576]{2,1,0:T(8,128)(2,1)S(1)}, u32[]{:S(2)}, u32[]{:S(2)}) collective-permute-start(bf16[2,48,576]{2,1,0:T(8,128)(2,1)S(1)} %fusion.47), channel_id=1, source_target_pairs={{0,4},{1,5},{2,6},{3,7},{4,0},{5,1},{6,2},{7,3},{8,12},{9,13},{10,... | collective-permute-start | bytes 331784 | tf_op jit(solution)/shard_map/ppermute | solution.py:174
  384.3 44.4 %collective-permute-start.29 = (bf16[48,1152]{1,0:T(8,128)(2,1)S(1)}, bf16[48,1152]{1,0:T(8,128)(2,1)S(1)}, u32[]{:S(2)}, u32[]{:S(2)}) collective-permute-start(bf16[48,1152]{1,0:T(8,128)(2,1)S(1)} %fusion.54), channel_id=1, source_target_pairs={{0,16},{16,0},{1,17},{17,1},{2,18},{18,2},{3,19},{19,3},{4,20},{20... | collective-permute-start | bytes 331784 | tf_op jit(solution)/shard_map/ppermute | solution.py:184
  384.9 5.2 %collective-permute-start.34 = (bf16[1,48,576]{2,1,0:T(8,128)(2,1)S(1)}, bf16[1,48,576]{2,1,0:T(8,128)(2,1)S(1)}, u32[]{:S(2)}, u32[]{:S(2)}) collective-permute-start(bf16[1,48,576]{2,1,0:T(8,128)(2,1)S(1)} %fusion.48), channel_id=1, source_target_pairs={{0,8},{1,9},{2,10},{3,11},{4,12},{5,13},{6,14},{7,15},{8,0},{9,1},... | collective-permute-start | bytes 165896 | tf_op jit(solution)/shard_map/ppermute | solution.py:174
  387.1 28.0 %collective-permute-start.42 = (bf16[8,48,1536]{2,1,0:T(8,128)(2,1)S(1)}, bf16[8,48,1536]{2,1,0:T(8,128)(2,1)S(1)}, u32[]{:S(2)}, u32[]{:S(2)}) collective-permute-start(bf16[8,48,1536]{2,1,0:T(8,128)(2,1)S(1)} %fusion.10), channel_id=1, source_target_pairs={{0,16},{16,0},{1,17},{17,1},{2,18},{18,2},{3,19},{19,3},{4,20},{20... | collective-permute-start | bytes 3538952 | tf_op jit(solution)/shard_map/ppermute | solution.py:180
  390.2 23.3 %collective-permute-start.35 = (bf16[48,576]{1,0:T(8,128)(2,1)S(1)}, bf16[48,576]{1,0:T(8,128)(2,1)S(1)}, u32[]{:S(2)}, u32[]{:S(2)}) collective-permute-start(bf16[48,576]{1,0:T(8,128)(2,1)S(1)} %fusion.57), channel_id=1, source_target_pairs={{0,16},{16,0},{1,17},{17,1},{2,18},{18,2},{3,19},{19,3},{4,20},{20... | collective-permute-start | bytes 165896 | tf_op jit(solution)/shard_map/ppermute | solution.py:184
  393.4 21.7 %copy-start.6 = (bf16[8,1,48,1536]{3,2,1,0:T(8,128)(2,1)S(1)}, bf16[8,1,48,1536]{3,2,1,0:T(8,128)(2,1)}, u32[]{:S(2)}) copy-start(bf16[8,1,48,1536]{3,2,1,0:T(8,128)(2,1)} %constant_dynamic-slice_fusion.12) | copy-start | bytes 3538948
  393.4 24.1 %collective-permute-start.48 = (bf16[4,192,768]{2,1,0:T(8,128)(2,1)S(1)}, bf16[4,192,768]{2,1,0:T(8,128)(2,1)S(1)}, u32[]{:S(2)}, u32[]{:S(2)}) collective-permute-start(bf16[4,192,768]{2,1,0:T(8,128)(2,1)S(1)} %fusion.12), channel_id=1, source_target_pairs={{0,2},{1,3},{2,0},{3,1},{4,6},{5,7},{6,4},{7,5},{8,10},{9,11},{10,... | collective-permute-start | bytes 3538952 | tf_op jit(solution)/shard_map/ppermute | solution.py:174
  415.1 13.4 %copy-start.12 = (bf16[4,1,48,1536]{3,2,1,0:T(8,128)(2,1)S(1)}, bf16[4,1,48,1536]{3,2,1,0:T(8,128)(2,1)}, u32[]{:S(2)}) copy-start(bf16[4,1,48,1536]{3,2,1,0:T(8,128)(2,1)} %constant_dynamic-slice_fusion.10) | copy-start | bytes 1769476
  415.3 13.2 %collective-permute-start.43 = (bf16[4,48,1536]{2,1,0:T(8,128)(2,1)S(1)}, bf16[4,48,1536]{2,1,0:T(8,128)(2,1)S(1)}, u32[]{:S(2)}, u32[]{:S(2)}) collective-permute-start(bf16[4,48,1536]{2,1,0:T(8,128)(2,1)S(1)} %fusion.19), channel_id=1, source_target_pairs={{0,2},{1,3},{2,0},{3,1},{4,6},{5,7},{6,4},{7,5},{8,10},{9,11},{10,... | collective-permute-start | bytes 1769480 | tf_op jit(solution)/shard_map/ppermute | solution.py:174
  417.7 20.9 %collective-permute-start.49 = (bf16[2,192,768]{2,1,0:T(8,128)(2,1)S(1)}, bf16[2,192,768]{2,1,0:T(8,128)(2,1)S(1)}, u32[]{:S(2)}, u32[]{:S(2)}) collective-permute-start(bf16[2,192,768]{2,1,0:T(8,128)(2,1)S(1)} %fusion.20), channel_id=1, source_target_pairs={{0,4},{1,5},{2,6},{3,7},{4,0},{5,1},{6,2},{7,3},{8,12},{9,13},{10,... | collective-permute-start | bytes 1769480 | tf_op jit(solution)/shard_map/ppermute | solution.py:174
  428.7 7.2 %collective-permute-start.44 = (bf16[2,48,1536]{2,1,0:T(8,128)(2,1)S(1)}, bf16[2,48,1536]{2,1,0:T(8,128)(2,1)S(1)}, u32[]{:S(2)}, u32[]{:S(2)}) collective-permute-start(bf16[2,48,1536]{2,1,0:T(8,128)(2,1)S(1)} %fusion.30), channel_id=1, source_target_pairs={{0,4},{1,5},{2,6},{3,7},{4,0},{5,1},{6,2},{7,3},{8,12},{9,13},{10,... | collective-permute-start | bytes 884744 | tf_op jit(solution)/shard_map/ppermute | solution.py:174
  436.0 13.1 %collective-permute-start.45 = (bf16[1,48,1536]{2,1,0:T(8,128)(2,1)S(1)}, bf16[1,48,1536]{2,1,0:T(8,128)(2,1)S(1)}, u32[]{:S(2)}, u32[]{:S(2)}) collective-permute-start(bf16[1,48,1536]{2,1,0:T(8,128)(2,1)S(1)} %fusion.32), channel_id=1, source_target_pairs={{0,8},{1,9},{2,10},{3,11},{4,12},{5,13},{6,14},{7,15},{8,0},{9,1},... | collective-permute-start | bytes 442376 | tf_op jit(solution)/shard_map/ppermute | solution.py:174
  438.7 15.1 %collective-permute-start.50 = (bf16[1,192,768]{2,1,0:T(8,128)(2,1)S(1)}, bf16[1,192,768]{2,1,0:T(8,128)(2,1)S(1)}, u32[]{:S(2)}, u32[]{:S(2)}) collective-permute-start(bf16[1,192,768]{2,1,0:T(8,128)(2,1)S(1)} %fusion.21), channel_id=1, source_target_pairs={{0,8},{1,9},{2,10},{3,11},{4,12},{5,13},{6,14},{7,15},{8,0},{9,1},... | collective-permute-start | bytes 884744 | tf_op jit(solution)/shard_map/ppermute | solution.py:174
  449.3 6.2 %collective-permute-start.46 = (bf16[48,1536]{1,0:T(8,128)(2,1)S(1)}, bf16[48,1536]{1,0:T(8,128)(2,1)S(1)}, u32[]{:S(2)}, u32[]{:S(2)}) collective-permute-start(bf16[48,1536]{1,0:T(8,128)(2,1)S(1)} %fusion.42), channel_id=1, source_target_pairs={{0,16},{16,0},{1,17},{17,1},{2,18},{18,2},{3,19},{19,3},{4,20},{20... | collective-permute-start | bytes 442376 | tf_op jit(solution)/shard_map/ppermute | solution.py:184
  454.0 7.4 %collective-permute-start.51 = (bf16[192,768]{1,0:T(8,128)(2,1)S(1)}, bf16[192,768]{1,0:T(8,128)(2,1)S(1)}, u32[]{:S(2)}, u32[]{:S(2)}) collective-permute-start(bf16[192,768]{1,0:T(8,128)(2,1)S(1)} %fusion.31), channel_id=1, source_target_pairs={{0,16},{16,0},{1,17},{17,1},{2,18},{18,2},{3,19},{19,3},{4,20},{20... | collective-permute-start | bytes 884744 | tf_op jit(solution)/shard_map/ppermute | solution.py:184
  (30 other events, 130.6 us)
where the time goes:
time: 471 us; the launch traced here: 463 us
  waiting for transfers between devices  173 us (37%)
  matrix products  97.4 us (21%)
  other arithmetic  58.2 us (12%)
  local copies, waits for them, and re-layouts  55.3 us (12%)
  starting transfers between devices  47.4 us (10%)
  Pallas kernels  29 us (6%)
    ppermute x20, waiting for transfers between devices, gather_blocks(): other = lax.ppermute(held, 'fsdp', swap_bit(count, bit))  89.1 us
    ppermute x24, waiting for transfers between devices, reduce_stages(): terms = home + [lax.ppermute(sent, 'fsdp', swap_bit(count, bit))]  53.3 us
    dot_general x4, matrix products, times_transpose(): lax.dot_general(left, right, (((1,), (1,)), ((), ())), preferred_element_...  39.8 us
    ppermute x6, waiting for transfers between devices, reduce_stages(): other = lax.ppermute(low, 'rep', cross)  30.9 us
    dot_general x4, matrix products, contract_rows(): lax.dot_general(left, right, (((0,), (0,)), ((), ())), preferred_element_...  28.1 us
    another operation x35, other arithmetic, gather_blocks(): jnp.stack(pair, axis=1).reshape((2 * held.shape[0],) + held.shape[1:])  20.9 us
    ppermute x20, starting transfers between devices, gather_blocks(): other = lax.ppermute(held, 'fsdp', swap_bit(count, bit))  19 us
    pallas_call x1, Pallas kernels, attend_backward(): pl.pallas_call(attend_backward_body, grid=(seqs,), in_specs=[pl.BlockSpec...  18.6 us
  transfers between devices with their start and end apart: 52, of which 27 were waited for; matrix products, arithmetic and copies ran while one was open for 23% of the time, Pallas kernels for 2%

commit v1 on v0

--- a/solution.py
+++ b/solution.py
@@ -146,6 +146,56 @@
     )(projected, attend, d_context)
 
 
+def inner_backward_body(
+    d_out_ref, normed_ref, slope_ref, down_ref, in_ref,
+    grad_in_ref, bias_ref, d_normed_ref,
+):
+    d_out = d_out_ref[...]
+    d_inner = low_dot(d_out, down_ref[...], ((1,), (1,))) * slope_ref[...].astype(jnp.float32)
+    bias_ref[...] = jnp.sum(d_inner, axis=0, keepdims=True)
+    d_inner = d_inner.astype(jnp.bfloat16)
+    grad_in_ref[...] = low_dot(normed_ref[...], d_inner, ((0,), (0,))).astype(jnp.bfloat16)
+    back = low_dot(d_inner, in_ref[...], ((1,), (1,)))
+
+    @pl.when(pl.program_id(0) == 0)
+    def _():
+        d_normed_ref[...] = back
+
+    @pl.when(pl.program_id(0) > 0)
+    def _():
+        d_normed_ref[...] += back
+
+
+def inner_backward(d_out, normed, slope, full_down, full_in):
+    rows, width = d_out.shape
+    inner = slope.shape[1]
+    tile = 512
+    whole = pl.BlockSpec((rows, width), lambda step: (0, 0))
+    columns = pl.BlockSpec((rows, tile), lambda step: (0, step))
+    return pl.pallas_call(
+        inner_backward_body,
+        grid=(inner // tile,),
+        in_specs=[
+            whole,
+            whole,
+            columns,
+            pl.BlockSpec((tile, width), lambda step: (step, 0)),
+            pl.BlockSpec((width, tile), lambda step: (0, step)),
+        ],
+        out_specs=[
+            pl.BlockSpec((width, tile), lambda step: (0, step)),
+            pl.BlockSpec((1, tile), lambda step: (0, step)),
+            whole,
+        ],
+        out_shape=[
+            jax.ShapeDtypeStruct((width, inner), jnp.bfloat16),
+            jax.ShapeDtypeStruct((1, inner), jnp.float32),
+            jax.ShapeDtypeStruct((rows, width), jnp.float32),
+        ],
+        name="inner_backward",
+    )(d_out, normed, slope, full_down, full_in)
+
+
 def swap_bit(count, bit):
     return [(place, place ^ (1 << bit)) for place in range(count)]
 
@@ -213,16 +263,25 @@
     return own_big, pieces
 
 
-def gather_blocks(shard):
+def gather_blocks(shards):
     count = lax.axis_size("fsdp")
     place = lax.axis_index("fsdp")
-    held = shard[None]
+    held = jnp.concatenate(shards, axis=1)[None]
+    whole = []
     for bit in reversed(range(count.bit_length() - 1)):
         other = lax.ppermute(held, "fsdp", swap_bit(count, bit))
         upper = ((place >> bit) & 1) == 1
-        pair = [jnp.where(upper, other, held), jnp.where(upper, held, other)]
-        held = jnp.stack(pair, axis=1).reshape((2 * held.shape[0],) + held.shape[1:])
-    return held
+        widths = [shard.shape[1] for shard in shards] if bit == 0 else [held.shape[-1]]
+        start, joined = 0, []
+        for width in widths:
+            one = held[..., start : start + width]
+            two = other[..., start : start + width]
+            pair = [jnp.where(upper, two, one), jnp.where(upper, one, two)]
+            shape = (2 * held.shape[0], held.shape[1], width)
+            joined.append(jnp.stack(pair, axis=1).reshape(shape))
+            start += width
+        held, whole = joined[0], joined
+    return whole
 
 
 def gather_small(time_w2, parts):
@@ -231,7 +290,7 @@
     flat = jnp.concatenate([part.reshape(-1) for part in parts])
     rows = -(-flat.shape[0] // width)
     flat = jnp.pad(flat, (0, rows * width - flat.shape[0])).reshape(rows, width)
-    whole = gather_blocks(jnp.concatenate([time_w2, flat], axis=0))
+    (whole,) = gather_blocks([jnp.concatenate([time_w2, flat], axis=0)])
     full_tw2 = whole[:, : time_w2.shape[0]].reshape(-1, width)
     flat = whole[:, time_w2.shape[0] :].reshape(count, -1)
     pieces, start = [], 0
@@ -266,10 +325,13 @@
     full_gain = pieces[2].swapaxes(0, 1).reshape(norm_gains.shape[0], -1)
     full_ffb = pieces[3].reshape(-1)
     full_tb = pieces[4].reshape(-1)
-    full_qkv = gather_blocks(attn_qkv).reshape(-1, width_in)
-    full_out = gather_blocks(attn_out).reshape(-1, attn_out.shape[1])
-    full_in = gather_blocks(ff_in).reshape(-1, ff_in.shape[1])
-    full_down = gather_blocks(ff_out).reshape(-1, ff_out.shape[1])
+    (full_qkv,) = gather_blocks([attn_qkv])
+    full_qkv = full_qkv.reshape(-1, width_in)
+    full_out, full_in = gather_blocks([attn_out, ff_in])
+    full_out = full_out.reshape(-1, attn_out.shape[1])
+    full_in = full_in.reshape(-1, ff_in.shape[1])
+    (full_down,) = gather_blocks([ff_out])
+    full_down = full_down.reshape(-1, ff_out.shape[1])
     bias_rows = full_bias.astype(jnp.float32)
     gain_rows = full_gain.astype(jnp.float32)
     sinus = sinusoid(timesteps, full_tw1.shape[0])
@@ -309,13 +371,8 @@
     d_ffout_bias = jnp.sum(d_ff, axis=0)
     d_ff_low = d_ff.astype(jnp.bfloat16)
     grad_down = contract_rows(active_low, d_ff_low)
-    d_active = times_transpose(d_ff_low, full_down)
-    d_inner = d_active * slope_low.astype(jnp.float32)
-    d_ff_bias = jnp.sum(d_inner, axis=0)
-    d_inner_low = d_inner.astype(jnp.bfloat16)
-    grad_in = contract_rows(normed_low, d_inner_low)
-    d_normed = d_ff + times_transpose(d_inner_low, full_in)
-    d_attn, d_gain_one, d_shift_one = first_pull(d_normed)
+    grad_in, d_ff_bias, back = inner_backward(d_ff_low, normed_low, slope_low, full_down, full_in)
+    d_attn, d_gain_one, d_shift_one = first_pull(d_ff + back)
     d_out_bias = jnp.sum(d_attn, axis=0)
     d_attn_low = d_attn.astype(jnp.bfloat16)
     grad_out_proj = contract_rows(context_low, d_attn_low)
@@ -352,13 +409,10 @@
         return rows_in.reshape(rows_n, count, cols_n // count).swapaxes(0, 1).reshape(count, -1)
 
     share_down = reduce_matrix(grad_down)
-    share_in = reduce_matrix(grad_in, rep_first=True)
-    share_out = reduce_matrix(grad_out_proj)
-    middle = grad_qkv.shape[1] // 2
-    share_qkv = jnp.concatenate(
-        [reduce_matrix(grad_qkv[:, :middle]), reduce_matrix(grad_qkv[:, middle:], rep_first=True)],
-        axis=1,
-    )
+    mid_width = grad_in.shape[1]
+    share_mid = reduce_matrix(jnp.concatenate([grad_in, grad_out_proj], axis=1))
+    share_in, share_out = share_mid[:, :mid_width], share_mid[:, mid_width:]
+    share_qkv = reduce_matrix(grad_qkv, rep_first=True)
     share_tw2, pieces = reduce_small(
         grad_tw2,
         [

time: 471 us -> 470 us (level)
  matrix products: 97.4 us -> 54.4 us
  waiting for transfers between devices: 173 us -> 202 us
  Pallas kernels: 29 us -> 51.9 us
  local copies, waits for them, and re-layouts: 55.3 us -> 47.9 us
    ppermute x24 -> x16, waiting for transfers between devices: 53.3 us -> 85.6 us  [reduce_stages(): terms = home + [lax.ppermute(sent, 'fsdp', swap_bit(count, bit))]]
    dot_general x4 -> x2, matrix products: 39.8 us -> 10.9 us  [times_transpose(): lax.dot_general(left, right, (((1,), (1,)), ((), ())), preferred_element_...]
    ppermute x6 -> x4, waiting for transfers between devices: 30.9 us -> 7.2 us  [reduce_stages(): other = lax.ppermute(low, 'rep', cross)]
    pallas_call x0 -> x1, Pallas kernels: none -> 23 us  [inner_backward(): pl.pallas_call(inner_backward_body, grid=(inner // tile,), in_specs=[whol...]
    dot_general x4 -> x3, matrix products: 28.1 us -> 13 us  [contract_rows(): lax.dot_general(left, right, (((0,), (0,)), ((), ())), preferred_element_...]
    ppermute x2 -> x1, waiting for transfers between devices: 0.01 us -> 10.9 us  [reduce_stages(): terms = home + [lax.ppermute(sent, 'rep', cross)]]
    ppermute x20 -> x16, waiting for transfers between devices: 89.1 us -> 98.6 us  [gather_blocks(): other = lax.ppermute(held, 'fsdp', swap_bit(count, bit))]
    dynamic_slice x17 -> x10, local copies, waits for them, and re-layouts: 14.8 us -> 5.92 us  [reduce_stages(): lax.dynamic_index_in_dim(term, mine, 1, keepdims=False)]
  transfers between devices with their start and end apart: 52 -> 37, of which waited for: 27 -> 16; matrix products, arithmetic and copies ran while one was open for 23% -> 21% of each run, Pallas kernels for 2% -> 6%
where the time goes in v1:
time: 470 us; the launch traced here: 463 us
  waiting for transfers between devices  202 us (43%)
  other arithmetic  60.5 us (13%)
  matrix products  54.4 us (12%)
  Pallas kernels  51.9 us (11%)
  local copies, waits for them, and re-layouts  47.9 us (10%)
  starting transfers between devices  43.9 us (9%)
    ppermute x16, waiting for transfers between devices, gather_blocks(): other = lax.ppermute(held, 'fsdp', swap_bit(count, bit))  98.6 us
    ppermute x16, waiting for transfers between devices, reduce_stages(): terms = home + [lax.ppermute(sent, 'fsdp', swap_bit(count, bit))]  85.6 us
    pallas_call x1, Pallas kernels, inner_backward(): pl.pallas_call(inner_backward_body, grid=(inner // tile,), in_specs=[whol...  23 us
    ppermute x16, starting transfers between devices, reduce_stages(): terms = home + [lax.ppermute(sent, 'fsdp', swap_bit(count, bit))]  21.1 us
    pallas_call x1, Pallas kernels, attend_backward(): pl.pallas_call(attend_backward_body, grid=(seqs,), in_specs=[pl.BlockSpec...  18.4 us
    another operation x30, other arithmetic, gather_blocks(): joined.append(jnp.stack(pair, axis=1).reshape(shape))  17.4 us
    ppermute x16, starting transfers between devices, gather_blocks(): other = lax.ppermute(held, 'fsdp', swap_bit(count, bit))  14.6 us
    dot_general x1, matrix products, per_device(): jnp.dot(normed_low, full_in, preferred_element_type=jnp.float32)  13.5 us
  transfers between devices with their start and end apart: 37, of which 16 were waited for; matrix products, arithmetic and copies ran while one was open for 21% of the time, Pallas kernels for 6%

profile of v1, /device:TPU:0, one launch (start us, length us, event | category | flops | bytes accessed | tf_op | source)
XLA Modules:
  0.0 463.0 jit_solution(4119172177556890774)
XLA Ops:
  0.7 4.1 collective-permute-start.12
  5.9 2.9 collective-permute-start.4
  14.2 32.0 %collective-permute-done = bf16[1,39,768]{2,1,0:T(8,128)(2,1)S(1)} collective-permute-done((bf16[1,39,768]{2,1,0:T(8,128)(2,1)S(1)}, bf16[1,39,768]{2,1,0:T(8,128)(2,1)S(1)}, u32[]{:S(2)}, u32[]{:S(2)}) %collective-permute-start) | collective-permute-done | bytes 59936 | tf_op jit(solution)/shard_map/ppermute | solution.py:272
  49.2 2.8 collective-permute-done.1
  52.1 1.6 collective-permute-start.2
  59.4 8.4 %collective-permute-done.5 = bf16[2,48,2304]{2,1,0:T(8,128)(2,1)S(1)} collective-permute-done((bf16[2,48,2304]{2,1,0:T(8,128)(2,1)S(1)}, bf16[2,48,2304]{2,1,0:T(8,128)(2,1)S(1)}, u32[]{:S(2)}, u32[]{:S(2)}) %collective-permute-start.5) | collective-permute-done | bytes 442400 | tf_op jit(solution)/shard_map/ppermute | solution.py:272
  68.6 11.9 %collective-permute-done.13 = bf16[2,192,768]{2,1,0:T(8,128)(2,1)S(1)} collective-permute-done((bf16[2,192,768]{2,1,0:T(8,128)(2,1)S(1)}, bf16[2,192,768]{2,1,0:T(8,128)(2,1)S(1)}, u32[]{:S(2)}, u32[]{:S(2)}) %collective-permute-start.13) | collective-permute-done | bytes 589856 | tf_op jit(solution)/shard_map/ppermute | solution.py:272
  87.7 1.8 fusion.25
  90.9 2.7 collective-permute-done.9
  97.2 18.5 %collective-permute-done.14 = bf16[4,192,768]{2,1,0:T(8,128)(2,1)} collective-permute-done((bf16[4,192,768]{2,1,0:T(8,128)(2,1)S(1)}, bf16[4,192,768]{2,1,0:T(8,128)(2,1)}, u32[]{:S(2)}, u32[]{:S(2)}) %collective-permute-start.14) | collective-permute-done | bytes 1179680 | tf_op jit(solution)/shard_map/ppermute | solution.py:272
  115.7 1.4 select_bitcast_fusion.9
  117.4 1.6 copy.63
  119.0 22.1 %collective-permute-done.10 = bf16[4,48,3840]{2,1,0:T(8,128)(2,1)S(1)} collective-permute-done((bf16[4,48,3840]{2,1,0:T(8,128)(2,1)S(1)}, bf16[4,48,3840]{2,1,0:T(8,128)(2,1)S(1)}, u32[]{:S(2)}, u32[]{:S(2)}) %collective-permute-start.10) | collective-permute-done | bytes 1474592 | tf_op jit(solution)/shard_map/ppermute | solution.py:272
  142.9 1.7 copy-done.14
  144.6 5.6 %add_convert_fusion.projected_ref = bf16[1024,2304]{1,0:T(8,128)(2,1)} fusion(bf16[1024,768]{1,0:T(8,128)(2,1)S(1)} %bitcast.386, bf16[768,2304]{1,0:T(8,128)(2,1)S(1)} %bitcast.363, f32[2304]{0:T(1024)S(1)} %pad_maximum_fusion.13), kind=kOutput, calls=%fused_computation.8 | convolution fusion | flops 3628597248 | bytes 9839616 | tf_op jit(solution)/shard_map/dot_general | solution.py:344
  150.2 10.5 %attend_forward.1 = (bf16[1024,768]{1,0:T(8,128)(2,1)}, bf16[1024,1536]{1,0:T(8,128)(2,1)}) custom-call(bf16[1024,2304]{1,0:T(8,128)(2,1)} %add_convert_fusion.projected_ref), custom_call_target="tpu_custom_call" | custom-call | tf_op jit(solution)/shard_map/attend_forward/pallas_call | solution.py:76
  160.7 2.7 select_bitcast_fusion.1
  164.3 3.7 select_bitcast_fusion.3
  168.9 1.7 select_bitcast_fusion.17
  170.8 2.2 copy-done.4
  173.5 1.5 fusion.61
  176.1 13.5 %fusion.4 = (bf16[1024,3072]{1,0:T(8,128)(2,1)}, bf16[1024,3072]{1,0:T(8,128)(2,1)S(1)}) fusion(f32[3072]{0:T(1024)S(1)} %reshape.1058, bf16[1024,768]{1,0:T(8,128)(2,1)S(1)} %fusion.10.normed_ref, bf16[768,3072]{1,0:T(8,128)(2,1)S(1)} %bitcast.328), kind=kOutput, calls=%fused_computation.5 | convolution fusion | flops 4872732672 | bytes 18886656 | tf_op jit(solution)/shard_map/dot_general | solution.py:354
  189.7 5.4 %fusion.62 = (f32[1024]{0:T(1024)S(1)}, f32[1024,768]{1,0:T(8,128)S(1)}) fusion(f32[768]{0:T(1024)S(1)} %add.752, bf16[1024,3072]{1,0:T(8,128)(2,1)S(1)} %get-tuple-element.51, bf16[3072,768]{1,0:T(8,128)(2,1)S(1)} %bitcast.326, f32[768]{0:T(1024)S(1)} %add.744, f32[768]{0:T(1024)S(1)} %mul.223, f32[1024]{0:T(1024)S(1)} %fusion.48, ...), kind=kOutput, calls=%fused_computation.228 | convolution fusion | flops 4837342208 | bytes 17323008 | tf_op jit(solution)/shard_map/dot_general | solution.py:362
  198.9 2.5 fusion.59
  201.4 1.7 copy-done
  203.3 7.1 %convolution_convert_fusion = bf16[3072,768]{1,0:T(8,128)(2,1)} fusion(bf16[1024,3072]{1,0:T(8,128)(2,1)S(1)} %get-tuple-element.51, bf16[1024,768]{1,0:T(8,128)(2,1)S(1)} %convert_element_type.739.d_out_ref), kind=kOutput, calls=%fused_computation.13 | convolution fusion | flops 4834197504 | bytes 12582912 | tf_op jit(solution)/shard_map/dot_general | solution.py:31
  210.4 23.0 %inner_backward.1 = (bf16[768,3072]{1,0:T(8,128)(2,1)}, f32[1,3072]{1,0:T(1,128)}, f32[1024,768]{1,0:T(8,128)}) custom-call(bf16[1024,768]{1,0:T(8,128)(2,1)} %copy-done.9, bf16[1024,768]{1,0:T(8,128)(2,1)} %copy-done.8, bf16[1024,3072]{1,0:T(8,128)(2,1)} %get-tuple-element.50.slope_ref, bf16[3072,768]{1,0:T(8,128)(2,1)} %bitcast.327, ...), custom_call_target="tpu_custom_call" | custom-call | tf_op jit(solution)/shard_map/inner_backward/pallas_call | solution.py:175
  233.4 3.8 multiply_reduce_fusion
  239.1 1.5 convolution_convert_fusion.3
  241.6 2.6 convolution_convert_fusion.2.d_context_ref
  244.2 2.8 constant_dynamic-slice_fusion.1
  248.2 2.7 fusion.9
  251.4 18.4 %attend_backward.1 = (bf16[1024,2304]{1,0:T(8,128)(2,1)}, f32[8,2,768]{2,1,0:T(2,128)}) custom-call(bf16[1024,2304]{1,0:T(8,128)(2,1)} %add_convert_fusion.projected_ref, bf16[1024,1536]{1,0:T(8,128)(2,1)} %get-tuple-element.21.attend_ref, bf16[1024,768]{1,0:T(8,128)(2,1)} %convolution_convert_fusion.2.d_context_ref), custom_call_target="tpu_custom_call" | custom-call | tf_op jit(solution)/shard_map/attend_backward/pallas_call | solution.py:129
  269.8 8.3 %bitcast_reduce_fusion = (f32[8,768]{1,0:T(8,128)S(1)}, f32[1024,768]{1,0:T(8,128)S(1)}) fusion(f32[1024,768]{1,0:T(8,128)} %copy-done.18, bf16[1024,2304]{1,0:T(8,128)(2,1)} %get-tuple-element.22, bf16[768,2304]{1,0:T(8,128)(2,1)} %bitcast.364), kind=kOutput, calls=%fused_computation.18 | convolution fusion | flops 3625445376 | bytes 14573568 | tf_op jit(solution)/shard_map/dot_general | solution.py:37
  278.1 4.4 convolution_convert_fusion.1
  282.6 1.7 copy-done.15
  286.9 1.9 fusion.57
  290.0 1.5 convolution_convert_fusion.4
  292.1 1.6 constant_dynamic-slice_fusion.7
  294.6 7.3 %collective-permute-done.17 = bf16[4,39,768]{2,1,0:T(8,128)(2,1)S(1)} collective-permute-done((bf16[4,39,768]{2,1,0:T(8,128)(2,1)S(1)}, bf16[4,39,768]{2,1,0:T(8,128)(2,1)S(1)}, u32[]{:S(2)}, u32[]{:S(2)}) %collective-permute-start.17) | collective-permute-done | bytes 239648 | tf_op jit(solution)/shard_map/ppermute | solution.py:224
  302.0 2.5 collective-permute-start.18
  304.5 1.9 fusion.11
  306.4 1.6 collective-permute-start.22
  308.0 3.6 collective-permute-start.19
  313.9 1.6 collective-permute-start.20
  316.8 10.9 %collective-permute-done.22 = bf16[8,48,1152]{2,1,0:T(8,128)(2,1)S(1)} collective-permute-done((bf16[8,48,1152]{2,1,0:T(8,128)(2,1)S(1)}, bf16[8,48,1152]{2,1,0:T(8,128)(2,1)S(1)}, u32[]{:S(2)}, u32[]{:S(2)}) %collective-permute-start.22) | collective-permute-done | bytes 884768 | tf_op jit(solution)/shard_map/ppermute | solution.py:230
  328.4 1.7 fusion.12
  330.2 1.6 collective-permute-start.28
  331.8 1.6 fusion.14
  335.3 5.6 %collective-permute-done.23 = bf16[4,48,1152]{2,1,0:T(8,128)(2,1)S(1)} collective-permute-done((bf16[4,48,1152]{2,1,0:T(8,128)(2,1)S(1)}, bf16[4,48,1152]{2,1,0:T(8,128)(2,1)S(1)}, u32[]{:S(2)}, u32[]{:S(2)}) %collective-permute-start.23) | collective-permute-done | bytes 442400 | tf_op jit(solution)/shard_map/ppermute | solution.py:224
  341.5 1.5 constant_dynamic-slice_fusion.8
  343.0 5.2 %collective-permute-done.24 = bf16[2,48,1152]{2,1,0:T(8,128)(2,1)S(1)} collective-permute-done((bf16[2,48,1152]{2,1,0:T(8,128)(2,1)S(1)}, bf16[2,48,1152]{2,1,0:T(8,128)(2,1)S(1)}, u32[]{:S(2)}, u32[]{:S(2)}) %collective-permute-start.24) | collective-permute-done | bytes 221216 | tf_op jit(solution)/shard_map/ppermute | solution.py:224
  348.9 2.4 collective-permute-start.25
  351.2 43.1 %collective-permute-done.33 = bf16[4,192,768]{2,1,0:T(8,128)(2,1)S(1)} collective-permute-done((bf16[4,192,768]{2,1,0:T(8,128)(2,1)S(1)}, bf16[4,192,768]{2,1,0:T(8,128)(2,1)S(1)}, u32[]{:S(2)}, u32[]{:S(2)}) %collective-permute-start.33) | collective-permute-done | bytes 1179680 | tf_op jit(solution)/shard_map/ppermute | solution.py:224
  398.5 1.4 collective-permute-start.29
  412.8 1.7 collective-permute-start.26
  415.8 3.5 collective-permute-start.35
  419.2 11.5 %collective-permute-done.29 = bf16[2,48,3840]{2,1,0:T(8,128)(2,1)} collective-permute-done((bf16[2,48,3840]{2,1,0:T(8,128)(2,1)}, bf16[2,48,3840]{2,1,0:T(8,128)(2,1)}, u32[]{:S(2)}, u32[]{:S(2)}) %collective-permute-start.29) | collective-permute-done | bytes 737312 | tf_op jit(solution)/shard_map/ppermute | solution.py:224
  432.1 1.8 collective-permute-start.30
  435.3 1.7 collective-permute-start.36
  437.0 12.2 %collective-permute-done.30 = bf16[1,48,3840]{2,1,0:T(8,128)(2,1)S(1)} collective-permute-done((bf16[1,48,3840]{2,1,0:T(8,128)(2,1)S(1)}, bf16[1,48,3840]{2,1,0:T(8,128)(2,1)S(1)}, u32[]{:S(2)}, u32[]{:S(2)}) %collective-permute-start.30) | collective-permute-done | bytes 368672 | tf_op jit(solution)/shard_map/ppermute | solution.py:224
  449.2 1.4 fusion.30
  450.7 1.7 collective-permute-start.31
  454.1 7.2 %collective-permute-done.31 = bf16[48,3840]{1,0:T(8,128)(2,1)S(1)} collective-permute-done((bf16[48,3840]{1,0:T(8,128)(2,1)S(1)}, bf16[48,3840]{1,0:T(8,128)(2,1)S(1)}, u32[]{:S(2)}, u32[]{:S(2)}) %collective-permute-start.31) | collective-permute-done | bytes 368672 | tf_op jit(solution)/shard_map/ppermute | solution.py:234
  (291 shorter events, 78.9 us)
Async XLA Ops:
  0.6 55.2 %copy-start.28 = (bf16[192,768]{1,0:T(8,128)(2,1)S(1)}, bf16[192,768]{1,0:T(8,128)(2,1)}, u32[]{:S(2)}) copy-start(bf16[192,768]{1,0:T(8,128)(2,1)} %param.25) | copy-start | bytes 884740
  0.7 55.2 %collective-permute-start.12 = (bf16[1,192,768]{2,1,0:T(8,128)(2,1)}, bf16[1,192,768]{2,1,0:T(8,128)(2,1)S(1)}, u32[]{:S(2)}, u32[]{:S(2)}) collective-permute-start(bf16[1,192,768]{2,1,0:T(8,128)(2,1)} %bitcast.417), channel_id=1, source_target_pairs={{0,8},{1,9},{2,10},{3,11},{4,12},{5,13},{6,14},{7,15},{8,0},{9,1},... | collective-permute-start | bytes 884744 | tf_op jit(solution)/shard_map/ppermute | solution.py:272
  5.8 51.3 %copy-start.26 = (bf16[48,3072]{1,0:T(8,128)(2,1)S(1)}, bf16[48,3072]{1,0:T(8,128)(2,1)}, u32[]{:S(2)}) copy-start(bf16[48,3072]{1,0:T(8,128)(2,1)} %param.24) | copy-start | bytes 884740
  5.8 51.2 %copy-start.29 = (bf16[48,768]{1,0:T(8,128)(2,1)S(1)}, bf16[48,768]{1,0:T(8,128)(2,1)}, u32[]{:S(2)}) copy-start(bf16[48,768]{1,0:T(8,128)(2,1)} %param.23) | copy-start | bytes 221188
  5.8 51.2 %collective-permute-start.8 = (bf16[1,48,3840]{2,1,0:T(8,128)(2,1)S(1)}, bf16[1,48,3840]{2,1,0:T(8,128)(2,1)S(1)}, u32[]{:S(2)}, u32[]{:S(2)}) collective-permute-start(bf16[1,48,3840]{2,1,0:T(8,128)(2,1)S(1)} %maximum_bitcast_fusion.3), channel_id=1, source_target_pairs={{0,8},{1,9},{2,10},{3,11},{4,12},{5,13},{6,14},{7,15},{8,0},{9,1},... | collective-permute-start | bytes 1105928 | tf_op jit(solution)/shard_map/ppermute | solution.py:272
  5.9 47.8 %collective-permute-start.4 = (bf16[1,48,2304]{2,1,0:T(8,128)(2,1)}, bf16[1,48,2304]{2,1,0:T(8,128)(2,1)S(1)}, u32[]{:S(2)}, u32[]{:S(2)}) collective-permute-start(bf16[1,48,2304]{2,1,0:T(8,128)(2,1)} %bitcast.422), channel_id=1, source_target_pairs={{0,8},{1,9},{2,10},{3,11},{4,12},{5,13},{6,14},{7,15},{8,0},{9,1},... | collective-permute-start | bytes 663560 | tf_op jit(solution)/shard_map/ppermute | solution.py:272
  13.3 33.0 %collective-permute-start = (bf16[1,39,768]{2,1,0:T(8,128)(2,1)S(1)}, bf16[1,39,768]{2,1,0:T(8,128)(2,1)S(1)}, u32[]{:S(2)}, u32[]{:S(2)}) collective-permute-start(bf16[1,39,768]{2,1,0:T(8,128)(2,1)S(1)} %maximum_bitcast_fusion.5), channel_id=1, source_target_pairs={{0,8},{1,9},{2,10},{3,11},{4,12},{5,13},{6,14},{7,15},{8,0},{9,1},... | collective-permute-start | bytes 179720 | tf_op jit(solution)/shard_map/ppermute | solution.py:272
  47.1 4.9 %collective-permute-start.1 = (bf16[2,39,768]{2,1,0:T(8,128)(2,1)S(1)}, bf16[2,39,768]{2,1,0:T(8,128)(2,1)S(1)}, u32[]{:S(2)}, u32[]{:S(2)}) collective-permute-start(bf16[2,39,768]{2,1,0:T(8,128)(2,1)S(1)} %maximum_bitcast_fusion.4), channel_id=1, source_target_pairs={{0,4},{1,5},{2,6},{3,7},{4,0},{5,1},{6,2},{7,3},{8,12},{9,13},{10,... | collective-permute-start | bytes 359432 | tf_op jit(solution)/shard_map/ppermute | solution.py:272
  52.1 7.1 %collective-permute-start.2 = (bf16[4,39,768]{2,1,0:T(8,128)(2,1)S(1)}, bf16[4,39,768]{2,1,0:T(8,128)(2,1)S(1)}, u32[]{:S(2)}, u32[]{:S(2)}) collective-permute-start(bf16[4,39,768]{2,1,0:T(8,128)(2,1)S(1)} %bitcast.403), channel_id=1, source_target_pairs={{0,2},{1,3},{2,0},{3,1},{4,6},{5,7},{6,4},{7,5},{8,10},{9,11},{10,... | collective-permute-start | bytes 718856 | tf_op jit(solution)/shard_map/ppermute | solution.py:272
  54.8 13.1 %collective-permute-start.5 = (bf16[2,48,2304]{2,1,0:T(8,128)(2,1)S(1)}, bf16[2,48,2304]{2,1,0:T(8,128)(2,1)S(1)}, u32[]{:S(2)}, u32[]{:S(2)}) collective-permute-start(bf16[2,48,2304]{2,1,0:T(8,128)(2,1)S(1)} %maximum_bitcast_fusion.2), channel_id=1, source_target_pairs={{0,4},{1,5},{2,6},{3,7},{4,0},{5,1},{6,2},{7,3},{8,12},{9,13},{10,... | collective-permute-start | bytes 1327112 | tf_op jit(solution)/shard_map/ppermute | solution.py:272
  56.0 24.5 %collective-permute-start.13 = (bf16[2,192,768]{2,1,0:T(8,128)(2,1)S(1)}, bf16[2,192,768]{2,1,0:T(8,128)(2,1)S(1)}, u32[]{:S(2)}, u32[]{:S(2)}) collective-permute-start(bf16[2,192,768]{2,1,0:T(8,128)(2,1)S(1)} %maximum_bitcast_fusion.1), channel_id=1, source_target_pairs={{0,4},{1,5},{2,6},{3,7},{4,0},{5,1},{6,2},{7,3},{8,12},{9,13},{10,... | collective-permute-start | bytes 1769480 | tf_op jit(solution)/shard_map/ppermute | solution.py:272
  57.2 10.8 %copy-start.16 = (bf16[1,1,48,3840]{3,2,1,0:T(8,128)(2,1)}, bf16[1,1,48,3840]{3,2,1,0:T(8,128)(2,1)S(1)}, u32[]{:S(2)}) copy-start(bf16[1,1,48,3840]{3,2,1,0:T(8,128)(2,1)S(1)} %get-tuple-element.85) | copy-start | bytes 1105924
  58.2 35.5 %collective-permute-start.9 = (bf16[2,48,3840]{2,1,0:T(8,128)(2,1)}, bf16[2,48,3840]{2,1,0:T(8,128)(2,1)}, u32[]{:S(2)}, u32[]{:S(2)}) collective-permute-start(bf16[2,48,3840]{2,1,0:T(8,128)(2,1)} %maximum_bitcast_fusion), channel_id=1, source_target_pairs={{0,4},{1,5},{2,6},{3,7},{4,0},{5,1},{6,2},{7,3},{8,12},{9,13},{10,... | collective-permute-start | bytes 2211848 | tf_op jit(solution)/shard_map/ppermute | solution.py:272
  59.4 21.9 %collective-permute-start.3 = (bf16[8,39,768]{2,1,0:T(8,128)(2,1)S(1)}, bf16[8,39,768]{2,1,0:T(8,128)(2,1)S(1)}, u32[]{:S(2)}, u32[]{:S(2)}) collective-permute-start(bf16[8,39,768]{2,1,0:T(8,128)(2,1)S(1)} %bitcast.374), channel_id=1, source_target_pairs={{0,1},{1,0},{2,3},{3,2},{4,5},{5,4},{6,7},{7,6},{8,9},{9,8},{10,11... | collective-permute-start | bytes 1437704 | tf_op jit(solution)/shard_map/ppermute | solution.py:272
  68.0 27.5 %collective-permute-start.6 = (bf16[4,48,2304]{2,1,0:T(8,128)(2,1)S(1)}, bf16[4,48,2304]{2,1,0:T(8,128)(2,1)}, u32[]{:S(2)}, u32[]{:S(2)}) collective-permute-start(bf16[4,48,2304]{2,1,0:T(8,128)(2,1)S(1)} %bitcast.370), channel_id=1, source_target_pairs={{0,2},{1,3},{2,0},{3,1},{4,6},{5,7},{6,4},{7,5},{8,10},{9,11},{10,... | collective-permute-start | bytes 2654216 | tf_op jit(solution)/shard_map/ppermute | solution.py:272
  80.7 35.0 %collective-permute-start.14 = (bf16[4,192,768]{2,1,0:T(8,128)(2,1)S(1)}, bf16[4,192,768]{2,1,0:T(8,128)(2,1)}, u32[]{:S(2)}, u32[]{:S(2)}) collective-permute-start(bf16[4,192,768]{2,1,0:T(8,128)(2,1)S(1)} %bitcast.354), channel_id=1, source_target_pairs={{0,2},{1,3},{2,0},{3,1},{4,6},{5,7},{6,4},{7,5},{8,10},{9,11},{10,... | collective-permute-start | bytes 3538952 | tf_op jit(solution)/shard_map/ppermute | solution.py:272
  81.8 7.7 %copy-start.7 = (bf16[16,32,768]{2,1,0:T(8,128)(2,1)}, bf16[16,32,768]{2,1,0:T(8,128)(2,1)S(1)}, u32[]{:S(2)}) copy-start(bf16[16,32,768]{2,1,0:T(8,128)(2,1)S(1)} %slice.131) | copy-start | bytes 2359300
  89.5 5.3 %copy-start.3 = (f32[8,128,768]{2,1,0:T(8,128)}, f32[8,128,768]{2,1,0:T(8,128)S(1)}, u32[]{:S(2)}) copy-start(f32[8,128,768]{2,1,0:T(8,128)S(1)} %get-tuple-element.72) | copy-start | bytes 9437188
  89.6 4.1 copy-start.17
  95.0 46.1 %collective-permute-start.10 = (bf16[4,48,3840]{2,1,0:T(8,128)(2,1)S(1)}, bf16[4,48,3840]{2,1,0:T(8,128)(2,1)S(1)}, u32[]{:S(2)}, u32[]{:S(2)}) collective-permute-start(bf16[4,48,3840]{2,1,0:T(8,128)(2,1)S(1)} %bitcast.347), channel_id=1, source_target_pairs={{0,2},{1,3},{2,0},{3,1},{4,6},{5,7},{6,4},{7,5},{8,10},{9,11},{10,... | collective-permute-start | bytes 4423688 | tf_op jit(solution)/shard_map/ppermute | solution.py:272
  97.2 44.8 %collective-permute-start.7 = (bf16[8,48,2304]{2,1,0:T(8,128)(2,1)S(1)}, bf16[8,48,2304]{2,1,0:T(8,128)(2,1)S(1)}, u32[]{:S(2)}, u32[]{:S(2)}) collective-permute-start(bf16[8,48,2304]{2,1,0:T(8,128)(2,1)S(1)} %bitcast.338), channel_id=1, source_target_pairs={{0,1},{1,0},{2,3},{3,2},{4,5},{5,4},{6,7},{7,6},{8,9},{9,8},{10,11... | collective-permute-start | bytes 5308424 | tf_op jit(solution)/shard_map/ppermute | solution.py:272
  119.0 41.7 %collective-permute-start.15 = (bf16[8,192,768]{2,1,0:T(8,128)(2,1)}, bf16[8,192,768]{2,1,0:T(8,128)(2,1)}, u32[]{:S(2)}, u32[]{:S(2)}) collective-permute-start(bf16[8,192,768]{2,1,0:T(8,128)(2,1)} %bitcast.60), channel_id=1, source_target_pairs={{0,1},{1,0},{2,3},{3,2},{4,5},{5,4},{6,7},{7,6},{8,9},{9,8},{10,11... | collective-permute-start | bytes 7077896 | tf_op jit(solution)/shard_map/ppermute | solution.py:272
  141.8 22.4 %collective-permute-start.11 = (bf16[8,48,3840]{2,1,0:T(8,128)(2,1)S(1)}, bf16[8,48,3840]{2,1,0:T(8,128)(2,1)}, u32[]{:S(2)}, u32[]{:S(2)}) collective-permute-start(bf16[8,48,3840]{2,1,0:T(8,128)(2,1)S(1)} %bitcast.333), channel_id=1, source_target_pairs={{0,1},{1,0},{2,3},{3,2},{4,5},{5,4},{6,7},{7,6},{8,9},{9,8},{10,11... | collective-permute-start | bytes 8847368 | tf_op jit(solution)/shard_map/ppermute | solution.py:272
  164.2 25.4 %copy-start.1 = (bf16[8,2,192,768]{3,2,1,0:T(8,128)(2,1)}, bf16[8,2,192,768]{3,2,1,0:T(8,128)(2,1)S(1)}, u32[]{:S(2)}) copy-start(bf16[8,2,192,768]{3,2,1,0:T(8,128)(2,1)S(1)} %copy.64) | copy-start | bytes 14155780
  168.8 7.3 %copy-start.2 = (bf16[8,2,48,3072]{3,2,1,0:T(8,128)(2,1)}, bf16[8,2,48,3072]{3,2,1,0:T(8,128)(2,1)S(1)}, u32[]{:S(2)}) copy-start(bf16[8,2,48,3072]{3,2,1,0:T(8,128)(2,1)S(1)} %copy.61) | copy-start | bytes 14155780
  168.8 4.2 copy-start.4
  168.9 4.6 copy-start.35
  170.8 4.2 copy-start.24
  176.1 13.6 %copy-start.8 = (bf16[1024,768]{1,0:T(8,128)(2,1)}, bf16[1024,768]{1,0:T(8,128)(2,1)S(1)}, u32[]{:S(2)}) copy-start(bf16[1024,768]{1,0:T(8,128)(2,1)S(1)} %fusion.10.normed_ref) | copy-start | bytes 4718596
  203.3 7.1 %copy-start.9 = (bf16[1024,768]{1,0:T(8,128)(2,1)}, bf16[1024,768]{1,0:T(8,128)(2,1)S(1)}, u32[]{:S(2)}) copy-start(bf16[1024,768]{1,0:T(8,128)(2,1)S(1)} %convert_element_type.739.d_out_ref) | copy-start | bytes 4718596
  238.9 5.3 %slice-start.2 = ((s8[4718592]{0:T(1024)(128)(4,1)}), s8[4194304]{0:T(1024)(128)(4,1)S(1)}, s32[]{:S(2)}) async-start(s8[4718592]{0:T(1024)(128)(4,1)} %bitcast.358), calls=%async_computation.2 | async-start | bytes 8388608
  239.1 5.1 %slice-start.3 = ((s8[4718592]{0:T(1024)(128)(4,1)}), s8[524288]{0:T(1024)(128)(4,1)S(1)}, s32[]{:S(2)}) async-start(s8[4718592]{0:T(1024)(128)(4,1)} %bitcast.358), calls=%async_computation.3 | async-start | bytes 1048576
  244.2 4.0 slice-start.1
  247.0 84.8 %collective-permute-start.32 = (bf16[8,192,768]{2,1,0:T(8,128)(2,1)}, bf16[8,192,768]{2,1,0:T(8,128)(2,1)}, u32[]{:S(2)}, u32[]{:S(2)}) collective-permute-start(bf16[8,192,768]{2,1,0:T(8,128)(2,1)} %get-tuple-element.59), channel_id=1, source_target_pairs={{0,1},{1,0},{2,3},{3,2},{4,5},{5,4},{6,7},{7,6},{8,9},{9,8},{10,11... | collective-permute-start | bytes 7077896 | tf_op jit(solution)/shard_map/ppermute | solution.py:224
  250.9 77.5 %collective-permute-start.27 = (bf16[8,48,3840]{2,1,0:T(8,128)(2,1)}, bf16[8,48,3840]{2,1,0:T(8,128)(2,1)}, u32[]{:S(2)}, u32[]{:S(2)}) collective-permute-start(bf16[8,48,3840]{2,1,0:T(8,128)(2,1)} %get-tuple-element.53), channel_id=1, source_target_pairs={{0,1},{1,0},{2,3},{3,2},{4,5},{5,4},{6,7},{7,6},{8,9},{9,8},{10,11... | collective-permute-start | bytes 8847368 | tf_op jit(solution)/shard_map/ppermute | solution.py:224
  269.8 8.3 %copy-start.21 = (bf16[1024,768]{1,0:T(8,128)(2,1)S(1)}, bf16[1024,768]{1,0:T(8,128)(2,1)}, u32[]{:S(2)}) copy-start(bf16[1024,768]{1,0:T(8,128)(2,1)} %bitcast_convert_fusion) | copy-start | bytes 4718596
  269.8 8.3 %copy-start.34 = (bf16[1024,2304]{1,0:T(8,128)(2,1)S(1)}, bf16[1024,2304]{1,0:T(8,128)(2,1)}, u32[]{:S(2)}) copy-start(bf16[1024,2304]{1,0:T(8,128)(2,1)} %get-tuple-element.22) | copy-start | bytes 14155780
  285.6 18.9 %collective-permute-start.21 = (bf16[8,48,2304]{2,1,0:T(8,128)(2,1)}, bf16[8,48,2304]{2,1,0:T(8,128)(2,1)}, u32[]{:S(2)}, u32[]{:S(2)}) collective-permute-start(bf16[8,48,2304]{2,1,0:T(8,128)(2,1)} %dynamic-slice_bitcast_fusion.1), channel_id=1, source_target_pairs={{0,1},{1,0},{2,3},{3,2},{4,5},{5,4},{6,7},{7,6},{8,9},{9,8},{10,11... | collective-permute-start | bytes 5308424 | tf_op jit(solution)/shard_map/ppermute | solution.py:224
  291.5 2.3 collective-permute-start.16
  293.8 103.3 %copy-start.10 = (bf16[4,1,48,3840]{3,2,1,0:T(8,128)(2,1)}, bf16[4,1,48,3840]{3,2,1,0:T(8,128)(2,1)S(1)}, u32[]{:S(2)}) copy-start(bf16[4,1,48,3840]{3,2,1,0:T(8,128)(2,1)S(1)} %constant_dynamic-slice_fusion.2) | copy-start | bytes 4423684
  293.8 17.9 %copy-start.6 = (bf16[8,1,192,768]{3,2,1,0:T(8,128)(2,1)S(1)}, bf16[8,1,192,768]{3,2,1,0:T(8,128)(2,1)}, u32[]{:S(2)}) copy-start(bf16[8,1,192,768]{3,2,1,0:T(8,128)(2,1)} %get-tuple-element.58) | copy-start | bytes 7077892
  293.9 8.0 %collective-permute-start.17 = (bf16[4,39,768]{2,1,0:T(8,128)(2,1)S(1)}, bf16[4,39,768]{2,1,0:T(8,128)(2,1)S(1)}, u32[]{:S(2)}, u32[]{:S(2)}) collective-permute-start(bf16[4,39,768]{2,1,0:T(8,128)(2,1)S(1)} %fusion.32), channel_id=1, source_target_pairs={{0,2},{1,3},{2,0},{3,1},{4,6},{5,7},{6,4},{7,5},{8,10},{9,11},{10,... | collective-permute-start | bytes 718856 | tf_op jit(solution)/shard_map/ppermute | solution.py:224
  294.5 53.6 %copy-start.19 = (bf16[4,1,48,1152]{3,2,1,0:T(8,128)(2,1)}, bf16[4,1,48,1152]{3,2,1,0:T(8,128)(2,1)S(1)}, u32[]{:S(2)}) copy-start(bf16[4,1,48,1152]{3,2,1,0:T(8,128)(2,1)S(1)} %constant_dynamic-slice_fusion.6) | copy-start | bytes 1327108
  302.0 6.0 %collective-permute-start.18 = (bf16[2,39,768]{2,1,0:T(8,128)(2,1)S(1)}, bf16[2,39,768]{2,1,0:T(8,128)(2,1)S(1)}, u32[]{:S(2)}, u32[]{:S(2)}) collective-permute-start(bf16[2,39,768]{2,1,0:T(8,128)(2,1)S(1)} %fusion.37), channel_id=1, source_target_pairs={{0,4},{1,5},{2,6},{3,7},{4,0},{5,1},{6,2},{7,3},{8,12},{9,13},{10,... | collective-permute-start | bytes 359432 | tf_op jit(solution)/shard_map/ppermute | solution.py:224
  306.4 21.3 %collective-permute-start.22 = (bf16[8,48,1152]{2,1,0:T(8,128)(2,1)S(1)}, bf16[8,48,1152]{2,1,0:T(8,128)(2,1)S(1)}, u32[]{:S(2)}, u32[]{:S(2)}) collective-permute-start(bf16[8,48,1152]{2,1,0:T(8,128)(2,1)S(1)} %fusion.11), channel_id=1, source_target_pairs={{0,16},{16,0},{1,17},{17,1},{2,18},{18,2},{3,19},{19,3},{4,20},{20... | collective-permute-start | bytes 2654216 | tf_op jit(solution)/shard_map/ppermute | solution.py:230
  308.0 5.8 %collective-permute-start.19 = (bf16[1,39,768]{2,1,0:T(8,128)(2,1)S(1)}, bf16[1,39,768]{2,1,0:T(8,128)(2,1)S(1)}, u32[]{:S(2)}, u32[]{:S(2)}) collective-permute-start(bf16[1,39,768]{2,1,0:T(8,128)(2,1)S(1)} %fusion.38), channel_id=1, source_target_pairs={{0,8},{1,9},{2,10},{3,11},{4,12},{5,13},{6,14},{7,15},{8,0},{9,1},... | collective-permute-start | bytes 179720 | tf_op jit(solution)/shard_map/ppermute | solution.py:224
  311.8 82.6 %copy-start.11 = (bf16[4,1,192,768]{3,2,1,0:T(8,128)(2,1)}, bf16[4,1,192,768]{3,2,1,0:T(8,128)(2,1)S(1)}, u32[]{:S(2)}) copy-start(bf16[4,1,192,768]{3,2,1,0:T(8,128)(2,1)S(1)} %constant_dynamic-slice_fusion) | copy-start | bytes 3538948
  313.9 86.0 %collective-permute-start.20 = (bf16[39,768]{1,0:T(8,128)(2,1)S(1)}, bf16[39,768]{1,0:T(8,128)(2,1)S(1)}, u32[]{:S(2)}, u32[]{:S(2)}) collective-permute-start(bf16[39,768]{1,0:T(8,128)(2,1)S(1)} %fusion.42), channel_id=1, source_target_pairs={{0,16},{16,0},{1,17},{17,1},{2,18},{18,2},{3,19},{19,3},{4,20},{20... | collective-permute-start | bytes 179720 | tf_op jit(solution)/shard_map/ppermute | solution.py:234
  327.9 13.1 %collective-permute-start.23 = (bf16[4,48,1152]{2,1,0:T(8,128)(2,1)S(1)}, bf16[4,48,1152]{2,1,0:T(8,128)(2,1)S(1)}, u32[]{:S(2)}, u32[]{:S(2)}) collective-permute-start(bf16[4,48,1152]{2,1,0:T(8,128)(2,1)S(1)} %fusion.29), channel_id=1, source_target_pairs={{0,2},{1,3},{2,0},{3,1},{4,6},{5,7},{6,4},{7,5},{8,10},{9,11},{10,... | collective-permute-start | bytes 1327112 | tf_op jit(solution)/shard_map/ppermute | solution.py:224
  330.2 66.9 %collective-permute-start.28 = (bf16[4,48,3840]{2,1,0:T(8,128)(2,1)S(1)}, bf16[4,48,3840]{2,1,0:T(8,128)(2,1)S(1)}, u32[]{:S(2)}, u32[]{:S(2)}) collective-permute-start(bf16[4,48,3840]{2,1,0:T(8,128)(2,1)S(1)} %fusion.12), channel_id=1, source_target_pairs={{0,2},{1,3},{2,0},{3,1},{4,6},{5,7},{6,4},{7,5},{8,10},{9,11},{10,... | collective-permute-start | bytes 4423688 | tf_op jit(solution)/shard_map/ppermute | solution.py:224
  333.4 61.0 %collective-permute-start.33 = (bf16[4,192,768]{2,1,0:T(8,128)(2,1)S(1)}, bf16[4,192,768]{2,1,0:T(8,128)(2,1)S(1)}, u32[]{:S(2)}, u32[]{:S(2)}) collective-permute-start(bf16[4,192,768]{2,1,0:T(8,128)(2,1)S(1)} %fusion.14), channel_id=1, source_target_pairs={{0,2},{1,3},{2,0},{3,1},{4,6},{5,7},{6,4},{7,5},{8,10},{9,11},{10,... | collective-permute-start | bytes 3538952 | tf_op jit(solution)/shard_map/ppermute | solution.py:224
  335.3 61.2 %copy-start.13 = (bf16[4,1,192,768]{3,2,1,0:T(8,128)(2,1)}, bf16[4,1,192,768]{3,2,1,0:T(8,128)(2,1)S(1)}, u32[]{:S(2)}) copy-start(bf16[4,1,192,768]{3,2,1,0:T(8,128)(2,1)S(1)} %constant_dynamic-slice_fusion.9) | copy-start | bytes 3538948
  341.0 55.5 %copy-start.27 = (bf16[4,48,1152]{2,1,0:T(8,128)(2,1)}, bf16[4,48,1152]{2,1,0:T(8,128)(2,1)S(1)}, u32[]{:S(2)}) copy-start(bf16[4,48,1152]{2,1,0:T(8,128)(2,1)S(1)} %collective-permute-done.23) | copy-start | bytes 1327108
  341.1 7.0 %collective-permute-start.24 = (bf16[2,48,1152]{2,1,0:T(8,128)(2,1)S(1)}, bf16[2,48,1152]{2,1,0:T(8,128)(2,1)S(1)}, u32[]{:S(2)}, u32[]{:S(2)}) collective-permute-start(bf16[2,48,1152]{2,1,0:T(8,128)(2,1)S(1)} %fusion.33), channel_id=1, source_target_pairs={{0,4},{1,5},{2,6},{3,7},{4,0},{5,1},{6,2},{7,3},{8,12},{9,13},{10,... | collective-permute-start | bytes 663560 | tf_op jit(solution)/shard_map/ppermute | solution.py:224
  348.1 52.5 %copy-start.30 = (bf16[2,48,1152]{2,1,0:T(8,128)(2,1)}, bf16[2,48,1152]{2,1,0:T(8,128)(2,1)S(1)}, u32[]{:S(2)}) copy-start(bf16[2,48,1152]{2,1,0:T(8,128)(2,1)S(1)} %collective-permute-done.24) | copy-start | bytes 663556
  348.9 62.8 %collective-permute-start.25 = (bf16[1,48,1152]{2,1,0:T(8,128)(2,1)}, bf16[1,48,1152]{2,1,0:T(8,128)(2,1)}, u32[]{:S(2)}, u32[]{:S(2)}) collective-permute-start(bf16[1,48,1152]{2,1,0:T(8,128)(2,1)} %fusion.34), channel_id=1, source_target_pairs={{0,8},{1,9},{2,10},{3,11},{4,12},{5,13},{6,14},{7,15},{8,0},{9,1},... | collective-permute-start | bytes 331784 | tf_op jit(solution)/shard_map/ppermute | solution.py:224
  396.4 18.0 %copy-start.12 = (bf16[4,1,192,768]{3,2,1,0:T(8,128)(2,1)S(1)}, bf16[4,1,192,768]{3,2,1,0:T(8,128)(2,1)}, u32[]{:S(2)}) copy-start(bf16[4,1,192,768]{3,2,1,0:T(8,128)(2,1)} %copy-done.11) | copy-start | bytes 3538948
  396.4 18.0 %collective-permute-start.34 = (bf16[2,192,768]{2,1,0:T(8,128)(2,1)}, bf16[2,192,768]{2,1,0:T(8,128)(2,1)}, u32[]{:S(2)}, u32[]{:S(2)}) collective-permute-start(bf16[2,192,768]{2,1,0:T(8,128)(2,1)} %fusion.21), channel_id=1, source_target_pairs={{0,4},{1,5},{2,6},{3,7},{4,0},{5,1},{6,2},{7,3},{8,12},{9,13},{10,... | collective-permute-start | bytes 1769480 | tf_op jit(solution)/shard_map/ppermute | solution.py:224
  398.5 32.3 %collective-permute-start.29 = (bf16[2,48,3840]{2,1,0:T(8,128)(2,1)}, bf16[2,48,3840]{2,1,0:T(8,128)(2,1)}, u32[]{:S(2)}, u32[]{:S(2)}) collective-permute-start(bf16[2,48,3840]{2,1,0:T(8,128)(2,1)} %fusion.17), channel_id=1, source_target_pairs={{0,4},{1,5},{2,6},{3,7},{4,0},{5,1},{6,2},{7,3},{8,12},{9,13},{10,... | collective-permute-start | bytes 2211848 | tf_op jit(solution)/shard_map/ppermute | solution.py:224
  412.8 21.1 %collective-permute-start.26 = (bf16[48,1152]{1,0:T(8,128)(2,1)S(1)}, bf16[48,1152]{1,0:T(8,128)(2,1)S(1)}, u32[]{:S(2)}, u32[]{:S(2)}) collective-permute-start(bf16[48,1152]{1,0:T(8,128)(2,1)S(1)} %fusion.41), channel_id=1, source_target_pairs={{0,16},{16,0},{1,17},{17,1},{2,18},{18,2},{3,19},{19,3},{4,20},{20... | collective-permute-start | bytes 331784 | tf_op jit(solution)/shard_map/ppermute | solution.py:234
  415.8 18.2 %collective-permute-start.35 = (bf16[1,192,768]{2,1,0:T(8,128)(2,1)S(1)}, bf16[1,192,768]{2,1,0:T(8,128)(2,1)S(1)}, u32[]{:S(2)}, u32[]{:S(2)}) collective-permute-start(bf16[1,192,768]{2,1,0:T(8,128)(2,1)S(1)} %fusion.22), channel_id=1, source_target_pairs={{0,8},{1,9},{2,10},{3,11},{4,12},{5,13},{6,14},{7,15},{8,0},{9,1},... | collective-permute-start | bytes 884744 | tf_op jit(solution)/shard_map/ppermute | solution.py:224
  432.1 17.1 %collective-permute-start.30 = (bf16[1,48,3840]{2,1,0:T(8,128)(2,1)S(1)}, bf16[1,48,3840]{2,1,0:T(8,128)(2,1)S(1)}, u32[]{:S(2)}, u32[]{:S(2)}) collective-permute-start(bf16[1,48,3840]{2,1,0:T(8,128)(2,1)S(1)} %fusion.18), channel_id=1, source_target_pairs={{0,8},{1,9},{2,10},{3,11},{4,12},{5,13},{6,14},{7,15},{8,0},{9,1},... | collective-permute-start | bytes 1105928 | tf_op jit(solution)/shard_map/ppermute | solution.py:224
  435.3 17.8 %collective-permute-start.36 = (bf16[192,768]{1,0:T(8,128)(2,1)S(1)}, bf16[192,768]{1,0:T(8,128)(2,1)S(1)}, u32[]{:S(2)}, u32[]{:S(2)}) collective-permute-start(bf16[192,768]{1,0:T(8,128)(2,1)S(1)} %fusion.31), channel_id=1, source_target_pairs={{0,16},{16,0},{1,17},{17,1},{2,18},{18,2},{3,19},{19,3},{4,20},{20... | collective-permute-start | bytes 884744 | tf_op jit(solution)/shard_map/ppermute | solution.py:234
  450.7 10.6 %collective-permute-start.31 = (bf16[48,3840]{1,0:T(8,128)(2,1)S(1)}, bf16[48,3840]{1,0:T(8,128)(2,1)S(1)}, u32[]{:S(2)}, u32[]{:S(2)}) collective-permute-start(bf16[48,3840]{1,0:T(8,128)(2,1)S(1)} %fusion.30), channel_id=1, source_target_pairs={{0,16},{16,0},{1,17},{17,1},{2,18},{18,2},{3,19},{19,3},{4,20},{20... | collective-permute-start | bytes 1105928 | tf_op jit(solution)/shard_map/ppermute | solution.py:234
  (14 other events, 29.5 us)
